TPU v7x, 256 devices: a whole 4x4x8 slice. The times are simulated.
256 devices in a mesh: seq: 32 (over y, z), wide: 8 (over x, core).
Axes of the slice: x: 4, y: 4, z: 8, core: 2. Of those that a mesh axis runs over, the one named last changes fastest.
Arguments:
- queries: bfloat16 [16384, 4096], P('seq', 'wide'), may hold values from -500 to 500
- keys: bfloat16 [16384, 4096], P('seq', 'wide'), may hold values from -500 to 500
- values: bfloat16 [16384, 4096], P('seq', 'wide'), may hold values from -6 to 6
- log_decay: float32 [16384, 32], P('seq', 'wide'), may hold values from -0.8 to 0, as said below
- ridge: float32 [4096], P('wide'), may hold values from 0.05 to 2
- out_weight: bfloat16 [4096, 4096], P('wide'), may hold values from -0.09375 to 0.09375
Outputs:
- mixed: bfloat16 [16384, 4096], P(('seq', 'wide'))
Inputs may be any that keep to these rules, and one draw needn't show every extreme that they name: `log_decay`: negative.
All inputs are finite; a program needn't handle non-finite values.
Results may differ from a plain program's by a relative error of at most 0.0065.
Values sent between devices are 32-bit elements; how exact they have to be, the bound alone decides.
A program may use at most 128 MiB of HBM per device.

v0:
```python
import jax
import jax.numpy as jnp
from jax import lax
from jax.sharding import PartitionSpec as P

HD = 128
SPAN = 128
ITERS = 8


highest = lax.Precision.HIGHEST


def unit_rows(matrix, head_count, head_size):
    entries = matrix.astype(jnp.float32).reshape(matrix.shape[0], head_count, head_size)
    return entries * lax.rsqrt(jnp.sum(entries * entries, axis=-1, keepdims=True) + 1e-06)


def span_read(query, key_rows, value_rows, cumulative, state_h, state_g, ridge_rows):
    length = query.shape[-2]
    places = jnp.arange(length)
    causal = places[:, None] >= places[None, :]
    spread = cumulative[..., :, None] - cumulative[..., None, :]
    weight = jnp.where(causal, jnp.exp(jnp.where(causal, spread, 0.0)), 0.0)
    opening = jnp.exp(cumulative)[..., None]
    solved = jnp.zeros_like(query)
    residual = query
    direction = query
    norm_now = jnp.sum(residual * residual, axis=-1, keepdims=True)
    for sweep in range(ITERS):
        operate_scores = (
            jnp.einsum("...td,...sd->...ts", direction, key_rows, precision=highest) * weight
        )
        operate_carried = jnp.einsum("...td,...ed->...te", direction, state_h, precision=highest)
        local_part = jnp.einsum("...ts,...sd->...td", operate_scores, key_rows, precision=highest)
        image = opening * operate_carried + local_part + ridge_rows * direction
        alpha = norm_now / jnp.sum(direction * image, axis=-1, keepdims=True)
        solved = solved + alpha * direction
        residual = residual - alpha * image
        norm_next = jnp.sum(residual * residual, axis=-1, keepdims=True)
        direction = residual + norm_next / norm_now * direction
        norm_now = norm_next
    scores = jnp.einsum("...td,...sd->...ts", solved, key_rows, precision=highest) * weight
    carried = jnp.einsum("...td,...ed->...te", solved, state_g, precision=highest)
    return opening * carried + jnp.einsum(
        "...ts,...se->...te", scores, value_rows, precision=highest
    )


def span_summary(key_rows, value_rows, cumulative):
    closing = cumulative[..., -1]
    fading = jnp.exp(closing[..., None] - cumulative)[..., None]
    gram = jnp.einsum("...sd,...se->...de", key_rows * fading, key_rows, precision=highest)
    memory = jnp.einsum("...se,...sd->...ed", value_rows * fading, key_rows, precision=highest)
    return (closing, gram, memory)


def combine_memories(earlier, later):
    factor = jnp.exp(later[2])[:, None, None]
    return (factor * earlier[0] + later[0], factor * earlier[1] + later[1], earlier[2] + later[2])


def body(queries, keys, values, log_decay, ridge, out_weight):
    rows_dev = queries.shape[0]
    head_count = log_decay.shape[1]
    head_size = HD
    block_list = rows_dev // SPAN

    def arrange(entries):
        return entries.reshape(block_list, SPAN, head_count, head_size).transpose(2, 0, 1, 3)

    query_rows = arrange(unit_rows(queries, head_count, head_size))
    key_rows = arrange(unit_rows(keys, head_count, head_size))
    value_rows = arrange(values.astype(jnp.float32).reshape(rows_dev, head_count, head_size))
    cumulative = jnp.cumsum(
        log_decay.reshape(block_list, SPAN, head_count).transpose(2, 0, 1), axis=-1
    )
    ridge_rows = ridge.reshape(head_count, 1, 1, head_size)
    closing, gram, memory = span_summary(key_rows, value_rows, cumulative)

    def running_summation(carry, items):
        return (combine_memories(carry, items), carry)

    blank_state = jnp.zeros((head_count, head_size, head_size), jnp.float32)
    blank_decay = jnp.zeros((head_count,), jnp.float32)
    shard_resident_carry, before = lax.scan(
        running_summation,
        (blank_state, blank_state, blank_decay),
        (gram.transpose(1, 0, 2, 3), memory.transpose(1, 0, 2, 3), closing.T),
    )
    device_h, device_g, device_decay = shard_resident_carry
    preceding_memory_h, incoming_gram_matrix, before_decay = before
    totals = lax.all_gather(device_decay[None], "seq", axis=0, tiled=True)
    position = lax.axis_index("seq")
    inclusive = jnp.cumsum(totals, axis=0)
    exclusive = inclusive - totals
    mine = lax.dynamic_index_in_dim(exclusive, position, 0, keepdims=False)
    preceding_rows = (jnp.arange(totals.shape[0]) < position)[:, None]
    lags = mine[None, :] - inclusive
    weights = jnp.where(preceding_rows, jnp.exp(jnp.where(preceding_rows, lags, 0.0)), 0.0)
    added_h = jnp.einsum(
        "jh,jhde->hde",
        weights,
        lax.all_gather(device_h[None], "seq", axis=0, tiled=True),
        precision=highest,
    )
    added_g = jnp.einsum(
        "jh,jhde->hde",
        weights,
        lax.all_gather(device_g[None], "seq", axis=0, tiled=True),
        precision=highest,
    )
    lifted = jnp.exp(before_decay)[..., None, None]
    start_h = (lifted * added_h[None] + preceding_memory_h).transpose(1, 0, 2, 3)
    start_g = (lifted * added_g[None] + incoming_gram_matrix).transpose(1, 0, 2, 3)
    reads = span_read(query_rows, key_rows, value_rows, cumulative, start_h, start_g, ridge_rows)
    reads = reads.transpose(1, 2, 0, 3).reshape(rows_dev, head_count, head_size)
    normed = reads * lax.rsqrt(jnp.mean(reads * reads, axis=-1, keepdims=True) + 1e-06)
    normed = normed.reshape(rows_dev, head_count * head_size).astype(jnp.bfloat16)
    mixed = lax.psum_scatter(
        jnp.dot(normed, out_weight, preferred_element_type=jnp.float32),
        "wide",
        scatter_dimension=0,
        tiled=True,
    )
    return mixed.astype(jnp.bfloat16)


def solution(mesh):
    placed = (
        P("seq", "wide"),
        P("seq", "wide"),
        P("seq", "wide"),
        P("seq", "wide"),
        P("wide"),
        P("wide", None),
    )
    return jax.shard_map(
        body, mesh=mesh, in_specs=placed, out_specs=P(("seq", "wide"), None), check_vma=False
    )
```

profile of v0, /device:TPU:1, one launch (start us, length us, event | category | flops | bytes accessed | tf_op | source)
XLA Modules:
  0.0 367.5 jit_solution(1191460066784433861)
XLA Ops:
  12.7 1.9 reduce_sum.173
  15.6 2.3 fusion.10
  17.9 3.2 convolution_bitcast_fusion.1
  23.5 8.0 %while.21 = (s32[]{:T(128)}, f32[4,128,128]{2,1,0:T(8,128)S(1)}, f32[4,128,128]{2,1,0:T(8,128)S(1)}, f32[4]{0:T(128)S(1)}, f32[4,4,128,128]{3,2,1,0:T(8,128)}, /...) while((s32[]{:T(128)}, f32[4,128,128]{2,1,0:T(8,128)S(1)}, ...), condition=%wide.region_5.6_spmd.clone, body=%wide.region_4.5_spmd.clone.sunk | while | flops 524299 | bytes 2622221 | solution.py:86
  34.4 65.5 %all-reduce = f32[128]{0:T(128)S(1)} all-reduce(f32[128]{0:T(128)S(1)} %dynamic-update-slice), channel_id=2, replica_groups=mesh['seq'=32,'wide'=8] {'seq'}, use_global_device_ids=true, to_apply=%add | all-reduce | flops 128 | bytes 1024
  100.2 2.4 reshape.176
  102.6 2.2 convert_multiply_fusion.1
  107.1 1.6 copy.60
  108.8 3.0 convolution_multiply_fusion.15
  111.8 21.4 %all-gather.6.cloned.1.call-done = f32[128,128,128]{2,1,0:T(8,128)} async-done(((f32[4,128,128]{2,1,0:T(8,128)}), f32[128,128,128]{2,1,0:T(8,128)}) %all-gather.6.cloned.1.call-update) | async-done | bytes 8388624 | tf_op jit(solution)/shard_map/all_gather | solution.py:104
  133.3 12.0 %fusion.6 = f32[4,1,128,128]{3,1,2,0:T(1,128)S(1)} fusion(f32[32,4,1,1]{0,2,3,1:T(1,128)S(1)} %copy.109, f32[32,4,128,128]{3,2,1,0:T(8,128)} %bitcast.204), kind=kOutput, calls=%fused_computation.12 | convolution fusion | flops 25165824 | bytes 8651264 | tf_op jit(solution)/shard_map/jh,jhde->hde/dot_general | solution.py:101
  145.3 85.5 %all-gather.8.cloned.1.call-done = f32[128,128,128]{2,1,0:T(8,128)} async-done(((f32[4,128,128]{2,1,0:T(8,128)}), f32[128,128,128]{2,1,0:T(8,128)}) %all-gather.8.cloned.1.call-update) | async-done | bytes 8388624 | tf_op jit(solution)/shard_map/all_gather | solution.py:110
  230.8 12.3 %fusion.4 = f32[4,1,128,128]{3,1,2,0:T(1,128)S(1)} fusion(f32[32,4,1,1]{0,2,3,1:T(1,128)S(1)} %copy.109, f32[32,4,128,128]{3,2,1,0:T(8,128)} %bitcast.205), kind=kOutput, calls=%fused_computation.10 | convolution fusion | flops 25165824 | bytes 8651264 | tf_op jit(solution)/shard_map/jh,jhde->hde/dot_general | solution.py:107
  244.7 2.5 fusion.48
  247.7 2.1 convolution_multiply_fusion.13
  251.0 2.4 multiply_reduce_fusion.12
  254.1 2.1 convolution_multiply_fusion.11
  257.8 2.4 multiply_reduce_fusion.10
  260.6 2.1 convolution_multiply_fusion.9
  263.9 2.4 multiply_reduce_fusion.8
  266.8 2.1 convolution_multiply_fusion.7
  270.0 2.6 multiply_reduce_fusion.6
  273.0 2.1 convolution_multiply_fusion.5
  276.3 2.4 multiply_reduce_fusion.4
  279.1 2.1 convolution_multiply_fusion.3
  282.4 2.4 multiply_reduce_fusion.2
  285.5 2.3 convolution_multiply_fusion.1
  289.0 2.4 fusion.24
  292.7 2.1 convolution_multiply_fusion
  298.5 7.8 %fusion.70 = f32[512,4096]{1,0:T(8,128)} fusion(bf16[512,4096]{1,0:T(8,128)(2,1)} %param.13, f32[64,8,4,128]{3,2,1,0:T(4,128)S(1)} %bitcast.206, f32[64,8,4,128]{3,2,1,0:T(4,128)S(1)} %bitcast.207), kind=kOutput, calls=%fused_computation.138 | convolution fusion | flops 2148007936 | bytes 14680064 | tf_op jit(solution)/shard_map/dot_general | solution.py:121
  306.3 52.4 %reduce-scatter.2.cloned.1.call-done = f32[64,4096]{1,0:T(8,128)} async-done(((f32[512,4096]{1,0:T(8,128)}), f32[64,4096]{1,0:T(8,128)}) %reduce-scatter.2.cloned.1.call-update) | async-done | bytes 1048592 | tf_op jit(solution)/shard_map/reduce_scatter | solution.py:120
  358.7 2.1 convert_element_type.16
  (117 shorter events, 40.8 us)
Async XLA Ops:
  6.5 8.6 %copy-start.5 = (bf16[512,512]{1,0:T(8,128)(2,1)S(1)}, bf16[512,512]{1,0:T(8,128)(2,1)}, u32[]{:S(2)}) copy-start(bf16[512,512]{1,0:T(8,128)(2,1)} %param.10) | copy-start | bytes 1572868
  6.5 126.7 %all-gather.6.cloned.1.call-start = ((), (), s32[]{:S(2)}) async-start(), calls=%async_computation.2 | async-start | bytes 8650752 | tf_op jit(solution)/shard_map/all_gather | solution.py:104
  21.1 11.8 %copy-start.7 = (u32[256]{0:T(256)S(1)}, u32[256]{0:T(256)}, u32[]{:S(2)}) copy-start(u32[256]{0:T(256)} %constant.48) | copy-start | bytes 3076
  31.4 0.7 copy-start
  31.4 0.8 copy-start.1
  32.1 198.7 %all-gather.8.cloned.1.call-start = ((), (), s32[]{:S(2)}) async-start(), calls=%async_computation.3 | async-start | bytes 8650752 | tf_op jit(solution)/shard_map/all_gather | solution.py:110
  32.9 325.8 %reduce-scatter.2.cloned.1.call-start = ((), (), s32[]{:S(2)}) async-start(), calls=%async_computation.1 | async-start | bytes 9437184 | tf_op jit(solution)/shard_map/reduce_scatter | solution.py:120
  145.3 99.4 %copy-start.6 = (f32[512]{0:T(512)S(1)}, f32[512]{0:T(512)}, u32[]{:S(2)}) copy-start(f32[512]{0:T(512)} %param.12) | copy-start | bytes 6148
  230.8 12.3 %copy-start.3 = (f32[4,4,128,128]{3,2,1,0:T(8,128)S(1)}, f32[4,4,128,128]{3,2,1,0:T(8,128)}, u32[]{:S(2)}) copy-start(f32[4,4,128,128]{3,2,1,0:T(8,128)} %get-tuple-element.65) | copy-start | bytes 3145732
  230.8 12.4 %copy-start.4 = (f32[4,4,128,128]{3,2,1,0:T(8,128)S(1)}, f32[4,4,128,128]{3,2,1,0:T(8,128)}, u32[]{:S(2)}) copy-start(f32[4,4,128,128]{3,2,1,0:T(8,128)} %get-tuple-element.67) | copy-start | bytes 3145732
  230.8 13.9 %copy-start.2 = (f32[4,4,128,128]{3,2,1,0:T(8,128)S(1)}, f32[4,4,128,128]{3,2,1,0:T(8,128)}, u32[]{:S(2)}) copy-start(f32[4,4,128,128]{3,2,1,0:T(8,128)} %convolution_multiply_fusion.15) | copy-start | bytes 3145732
Sparse Core Ops, SparseCore 0:
  32.3 100.9 all-gather.5
  135.9 94.9 all-gather.7
  306.4 52.2 reduce-scatter.1
where the time goes:
time: 373 us; the launch traced here: 368 us
  waiting for transfers between devices  160 us (43%)
  matrix products  89.4 us (24%)
  blocking collectives  65.5 us (18%)
  other arithmetic  22.3 us (6%)
  local copies, waits for them, and re-layouts  15.6 us (4%)
  between operations  14.5 us (4%)
    all_gather x1, waiting for transfers between devices, body(): lax.all_gather(device_g[None], 'seq', axis=0, tiled=True)  85.5 us
    unnamed x1, blocking collectives  65.5 us
    reduce_scatter x1, waiting for transfers between devices, body(): lax.psum_scatter(jnp.dot(normed, out_weight, preferred_element_type=jnp.f...  52.4 us
    all_gather x1, waiting for transfers between devices, body(): lax.all_gather(device_h[None], 'seq', axis=0, tiled=True)  21.4 us
    dot_general x8, matrix products, span_read(): jnp.einsum('...ts,...sd->...td', operate_scores, key_rows, precision=high...  19.5 us
    dot_general x8, matrix products, span_read(): jnp.einsum('...td,...sd->...ts', direction, key_rows, precision=highest)  18.1 us
    dot_general x1, matrix products, body(): jnp.einsum('jh,jhde->hde', weights, lax.all_gather(device_g[None], 'seq',...  12.3 us
    dot_general x1, matrix products, body(): jnp.einsum('jh,jhde->hde', weights, lax.all_gather(device_h[None], 'seq',...  12 us
  transfers between devices with their start and end apart: 3, of which 3 were waited for; matrix products, arithmetic and copies ran while one was open for 7% of the time, Pallas kernels for 0%

commit v1 on v0

v1 whole, which is shorter than its diff:
```python
import functools

import jax
import jax.numpy as jnp
from jax import lax
from jax.experimental import pallas as pl
from jax.experimental.pallas import tpu as pltpu
from jax.sharding import PartitionSpec as P

MESH = pl.DeviceIdType.MESH
F32 = jnp.float32
BF16 = jnp.bfloat16
HD = 128
SPAN = 128
ITERS = 8
HL = 4
NJ = 4
NCH = 8
ORDER = (2, 1, 3, 0)
highest = lax.Precision.HIGHEST


def parts(value):
    high = value.astype(BF16)
    return high, (value - high.astype(F32)).astype(BF16)


def stacked(value):
    return jnp.concatenate(parts(value), axis=0)


def dot(a, b):
    return jnp.dot(a, b, preferred_element_type=F32)


def kernel(
    ny, nz, nx,
    q_ref, k_ref, v_ref, ld_ref, ridge_ref, w_hbm, o_ref,
    w_vm, st, buf1, tot, buf2, pre, lb, sdec, crow, w1, w2, k2, kt2, vt2, qt, ridge_m,
    a1, a2, xs, rs, ps, nm, pown, pout, pin, ra, rb, f1, f2,
    w_sem, z_send, z_recv, y_send, y_recv, p_send, p_recv, r_send, r_recv, f_send, f_recv,
):
    seq = lax.axis_index("seq")
    wide = lax.axis_index("wide")
    y, z = lax.div(seq, nz), lax.rem(seq, nz)
    x, c = lax.div(wide, 2), lax.rem(wide, 2)
    rows = HD // nz
    partner = x * 2 + (1 - c)
    right = lax.rem(x + 1, nx) * 2 + c
    left = lax.rem(x + nx - 1, nx) * 2 + c

    load_w = pltpu.make_async_copy(w_hbm, w_vm, w_sem)
    load_w.start()

    barrier = pltpu.get_barrier_semaphore()
    for step in range(1, nz):
        to = y * nz + lax.rem(z + step, nz)
        pl.semaphore_signal(barrier, inc=1, device_id=(to, wide), device_id_type=MESH)
    for step in range(1, ny):
        to = lax.rem(y + step, ny) * nz + z
        pl.semaphore_signal(barrier, inc=1, device_id=(to, wide), device_id_type=MESH)
    for to in (partner, right, left):
        pl.semaphore_signal(barrier, inc=1, device_id=(seq, to), device_id_type=MESH)

    place_r = lax.broadcasted_iota(jnp.int32, (SPAN, SPAN), 0)
    place_c = lax.broadcasted_iota(jnp.int32, (SPAN, SPAN), 1)
    lower = (place_r >= place_c).astype(F32)
    upper = (place_r <= place_c).astype(F32)
    ccols, norms = [], {}
    total = jnp.zeros((1, HL), F32)
    closings = []
    for j in range(NJ):
        decay = ld_ref[j * SPAN : (j + 1) * SPAN, :]
        ccol = jnp.dot(lower, decay, precision=highest, preferred_element_type=F32)
        ccols.append(ccol)
        crow[j, 0:HL, :] = lax.dot_general(
            decay, upper, (((0,), (0,)), ((), ())), precision=highest, preferred_element_type=F32
        )
        for h in range(HL):
            sdec[j, h : h + 1, :] = jnp.exp(jnp.broadcast_to(total[:, h : h + 1], (1, HD)))
        closing = ccol[SPAN - 1 : SPAN, :]
        closings.append(closing)
        total = total + closing
    group = lax.rem(place_r, rows)
    marks = jnp.zeros((HD, HD), F32)
    for h in range(HL):
        marks = jnp.where(group == h, jnp.broadcast_to(total[:, h : h + 1], (HD, HD)), marks)
    st[0] = marks

    for h in range(HL):
        hc = slice(h * HD, (h + 1) * HD)
        run = jnp.zeros((HD, HD), F32)
        for j in range(NJ):
            keys = k_ref[j * SPAN : (j + 1) * SPAN, hc]
            k2[j, h, :, 0:HD] = keys
            k2[j, h, :, HD : 2 * HD] = keys
            keyf = keys.astype(F32)
            norm = lax.rsqrt(jnp.sum(keyf * keyf, axis=1, keepdims=True) + 1e-06)
            norms[j, h] = norm
            keyt = keyf.T.astype(BF16)
            kt2[j, h, :, 0:HD] = keyt
            kt2[j, h, :, HD : 2 * HD] = keyt
            fade = jnp.exp(closings[j][:, h : h + 1] - ccols[j][:, h : h + 1])
            gram = dot(kt2[j, h], stacked(keyf * (fade * norm * norm)))
            lb[j, h] = run
            run = jnp.exp(closings[j][:, h : h + 1]) * run + gram
        st[1 + h] = run

    pl.semaphore_wait(barrier, nz + ny + 1)

    def z_copy(src, dst, slot, step):
        to = y * nz + lax.rem(z + step, nz)
        return pltpu.make_async_remote_copy(
            src_ref=src, dst_ref=dst, send_sem=z_send.at[slot, step], recv_sem=z_recv.at[slot, step],
            device_id=(to, wide), device_id_type=MESH,
        )

    bands = ((0, HL + 1), (HL + 1, 2 * HL + 1))

    def scatter(band):
        lo, hi = bands[band]
        copies = []
        for step in range(1, nz):
            peer = lax.rem(z + step, nz)
            start = pl.multiple_of(peer * rows, rows)
            copies.append(z_copy(st.at[lo:hi, pl.ds(start, rows), :], buf1.at[z, lo:hi], band, step))
            copies[-1].start()
        mine = pl.multiple_of(z * rows, rows)
        buf1[z, lo:hi] = st[lo:hi, pl.ds(mine, rows), :]
        return copies

    sends = scatter(0)
    sent = list(sends)

    for h in range(HL):
        hc = slice(h * HD, (h + 1) * HD)
        run = jnp.zeros((HD, HD), F32)
        for j in range(NJ):
            keyf = k_ref[j * SPAN : (j + 1) * SPAN, hc].astype(F32)
            valt = v_ref[j * SPAN : (j + 1) * SPAN, hc].astype(F32).T.astype(BF16)
            vt2[j, h, :, 0:HD] = valt
            vt2[j, h, :, HD : 2 * HD] = valt
            fade = jnp.exp(closings[j][:, h : h + 1] - ccols[j][:, h : h + 1])
            memory = dot(vt2[j, h], stacked(keyf * (fade * norms[j, h])))
            lb[j, HL + h] = run
            run = jnp.exp(closings[j][:, h : h + 1]) * run + memory
        st[1 + HL + h] = run
    g_sends = scatter(1)
    sent += g_sends

    def row_total(band, copies):
        for copy in copies:
            copy.wait_recv()
        lo, hi = bands[band]
        first = 1 + band * HL
        sums = [jnp.zeros((rows, HD), F32) for _ in range(HL)]
        decay = jnp.zeros((8, HD), F32)
        for other in range(nz):
            marks = buf1[other, 0, 0:8, :]
            factor = jnp.exp(marks)
            decay = decay + marks
            for h in range(HL):
                sums[h] = factor[h : h + 1] * sums[h] + buf1[other, first + h]
        for h in range(HL):
            tot[y, first + h] = sums[h]
        if band == 0:
            tot[y, 0] = jnp.zeros((rows, HD), F32)
            tot[y, 0, 0:8, :] = decay
        copies = []
        for step in range(1, ny):
            to = lax.rem(y + step, ny) * nz + z
            copies.append(
                pltpu.make_async_remote_copy(
                    src_ref=tot.at[y, lo:hi], dst_ref=tot.at[y, lo:hi],
                    send_sem=y_send.at[band, step], recv_sem=y_recv.at[band, step],
                    device_id=(to, wide), device_id_type=MESH,
                )
            )
            copies[-1].start()
        return copies

    def give_back(band, copies):
        for copy in copies:
            copy.wait_recv()
        first = 1 + band * HL
        runs = [jnp.zeros((rows, HD), F32) for _ in range(HL)]
        for other in range(ny):
            factor = jnp.exp(tot[other, 0, 0:8, :])
            for h in range(HL):
                runs[h] = jnp.where(other < y, factor[h : h + 1] * runs[h] + tot[other, first + h], runs[h])
        for other in range(nz):
            factor = jnp.exp(buf1[other, 0, 0:8, :])
            for h in range(HL):
                buf2[other, band * HL + h] = runs[h]
                runs[h] = factor[h : h + 1] * runs[h] + buf1[other, first + h]
        lo, hi = band * HL, (band + 1) * HL
        mine = pl.multiple_of(z * rows, rows)
        copies = []
        for step in range(1, nz):
            peer = lax.rem(z + step, nz)
            copies.append(z_copy(buf2.at[peer, lo:hi], pre.at[lo:hi, pl.ds(mine, rows), :], 2 + band, step))
            copies[-1].start()
        pre[lo:hi, pl.ds(mine, rows), :] = buf2[z, lo:hi]
        return copies

    for h in range(HL):
        hc = slice(h * HD, (h + 1) * HD)
        ridge_m[h] = jnp.broadcast_to(ridge_ref[:, hc], (HD, HD)).T
        a1[h, 2 * HD : 3 * HD, HD : 2 * HD] = jnp.zeros((HD, HD), BF16)
        a2[h, 2 * HD : 3 * HD, HD : 2 * HD] = jnp.zeros((HD, HD), BF16)

    def weights_of(j):
        for h in range(HL):
            hc = slice(h * HD, (h + 1) * HD)
            lag = crow[j, h : h + 1, :] - ccols[j][:, h : h + 1]
            causal = place_r <= place_c
            weight = jnp.where(causal, jnp.exp(jnp.where(causal, lag, 0.0)), 0.0) * norms[j, h]
            w1[j, h] = weight
            w2[j, h] = weight * norms[j, h]
            query = q_ref[j * SPAN : (j + 1) * SPAN, hc].astype(F32).T
            qt[j, h] = query * lax.rsqrt(jnp.sum(query * query, axis=0, keepdims=True) + 1e-06)

    weights_of(0)
    weights_of(1)
    y_sends = row_total(0, sends)
    weights_of(2)
    back = give_back(0, y_sends)
    sent += y_sends + back
    y_sends = row_total(1, g_sends)
    weights_of(3)
    g_back = give_back(1, y_sends)
    sent += y_sends + g_back
    for copy in back:
        copy.wait_recv()

    def system(ref, j, h, state):
        high, low = parts(state)
        ref[h, 0:HD, :] = k2[j, h]
        ref[h, HD : 2 * HD, 0:HD] = high
        ref[h, HD : 2 * HD, HD : 2 * HD] = high
        ref[h, 2 * HD : 3 * HD, 0:HD] = low

    def solve(j):
        norm0, opening = [], []
        for h in range(HL):
            system(a1, j, h, sdec[j, h : h + 1, :] * pre[h] + lb[j, h])
            query = qt[j, h]
            xs[h] = jnp.zeros((HD, SPAN), F32)
            rs[h] = query
            ps[h] = query
            norm0.append(jnp.sum(query * query, axis=0, keepdims=True))
            opening.append(jnp.exp(crow[j, h : h + 1, :]))

        def sweep(_, norm):
            after = []
            for h in range(HL):
                direction = ps[h]
                out = dot(a1[h], stacked(direction))
                scores = out[0:HD] * w2[j, h]
                image = (
                    opening[h] * (out[HD : 2 * HD] + out[2 * HD : 3 * HD])
                    + dot(kt2[j, h], stacked(scores))
                    + ridge_m[h] * direction
                )
                alpha = norm[h] / jnp.sum(direction * image, axis=0, keepdims=True)
                xs[h] = xs[h] + alpha * direction
                residual = rs[h] - alpha * image
                fresh = jnp.sum(residual * residual, axis=0, keepdims=True)
                rs[h] = residual
                ps[h] = residual + (fresh / norm[h]) * direction
                after.append(fresh)
            return tuple(after)

        lax.fori_loop(0, ITERS, sweep, tuple(norm0))
        return opening

    def finish(j, opening):
        for h in range(HL):
            system(a2, j, h, sdec[j, h : h + 1, :] * pre[HL + h] + lb[j, HL + h])
            out = dot(a2[h], stacked(xs[h]))
            scores = out[0:HD] * w1[j, h]
            read = opening[h] * (out[HD : 2 * HD] + out[2 * HD : 3 * HD]) + dot(vt2[j, h], stacked(scores))
            read = read * lax.rsqrt(jnp.sum(read * read, axis=0, keepdims=True) * (1.0 / HD) + 1e-06)
            nm[:, h * HD : (h + 1) * HD] = read.T.astype(BF16)

    half = SPAN // 2
    width = w_vm.shape[1] // NCH

    def p_copy(k, n):
        return pltpu.make_async_remote_copy(
            src_ref=pout.at[k, n], dst_ref=pin.at[k, n], send_sem=p_send.at[k, n], recv_sem=p_recv.at[k, n],
            device_id=(seq, partner), device_id_type=MESH,
        )

    def project(k, first):
        mine = pl.multiple_of(c * half, half)
        other = pl.multiple_of((1 - c) * half, half)
        lhs = jnp.concatenate([nm[pl.ds(mine, half), :], nm[pl.ds(other, half), :]], axis=0)
        copies = {}
        for i in range(NCH):
            n = (first + i) % NCH
            out = dot(lhs, w_vm[:, n * width : (n + 1) * width])
            pown[k, n] = out[0:half]
            pout[k, n] = out[half:]
            copies[n] = p_copy(k, n)
            copies[n].start()
        return copies

    def x_copy(src, dst, send, recv, to):
        copy = pltpu.make_async_remote_copy(
            src_ref=src, dst_ref=dst, send_sem=send, recv_sem=recv,
            device_id=(seq, to), device_id_type=MESH,
        )
        copy.start()
        return copy

    middle = NCH // 2
    js = [lax.rem(x + o, nx) for o in ORDER]

    opening = solve(js[0])
    for copy in g_back:
        copy.wait_recv()
    finish(js[0], opening)
    load_w.wait()
    copies = project(0, 0)
    relay = {}
    for i in range(NCH):
        n = (i % 2) * middle + i // 2
        copies[n].wait_recv()
        pown[0, n] = pown[0, n] + pin[0, n]
        if n < middle:
            relay[n] = x_copy(pown.at[0, n], ra.at[n], r_send.at[n], r_recv.at[n], right)
        else:
            relay[n] = x_copy(pown.at[0, n], rb.at[n - middle], r_send.at[n], r_recv.at[n], left)
    sent += list(copies.values()) + list(relay.values())

    final1, final2 = {}, {}
    opening = solve(js[1])
    finish(js[1], opening)
    copies1 = project(1, middle)
    for n in range(middle, NCH):
        copies1[n].wait_recv()
        pown[1, n] = pown[1, n] + pin[1, n]
        final1[n] = x_copy(pown.at[1, n], f1.at[n], f_send.at[0, n], f_recv.at[0, n], right)
    opening = solve(js[2])
    finish(js[2], opening)
    copies2 = project(2, 0)
    for n in range(middle):
        copies2[n].wait_recv()
        pown[2, n] = pown[2, n] + pin[2, n]
        final2[n] = x_copy(pown.at[2, n], f2.at[n], f_send.at[1, n], f_recv.at[1, n], left)
    for n in range(middle):
        copies1[n].wait_recv()
        relay[n].wait_recv()
        pown[1, n] = pown[1, n] + pin[1, n] + ra[n]
        final1[n] = x_copy(pown.at[1, n], f1.at[n], f_send.at[0, n], f_recv.at[0, n], right)
        m = n + middle
        copies2[m].wait_recv()
        relay[m].wait_recv()
        pown[2, m] = pown[2, m] + pin[2, m] + rb[n]
        final2[m] = x_copy(pown.at[2, m], f2.at[m], f_send.at[1, m], f_recv.at[1, m], left)
    sent += list(copies1.values()) + list(copies2.values()) + list(final1.values()) + list(final2.values())

    opening = solve(js[3])
    finish(js[3], opening)
    copies3 = project(3, 0)
    sent += list(copies3.values())
    for n in range(NCH):
        copies3[n].wait_recv()
        pown[3, n] = pown[3, n] + pin[3, n]
    for i in range(NCH):
        n = (i % 2) * middle + i // 2
        m = (n + middle) % NCH
        final1[m].wait_recv()
        final2[n].wait_recv()
        if i % 2 == 1:
            for e in (n, m):
                o_ref[:, e * width : (e + 1) * width] = (pown[3, e] + f1[e] + f2[e]).astype(BF16)
    for copy in sent:
        copy.wait_send()


def solution(mesh, ny=4, nz=8):
    nx = mesh.shape["wide"] // 2

    def body(queries, keys, values, log_decay, ridge, out_weight):
        columns = out_weight.shape[1]
        width = columns // NCH
        half = SPAN // 2
        rows = HD // nz
        vm = pltpu.VMEM
        dma = pltpu.SemaphoreType.DMA
        scratch = [
            vm(out_weight.shape, BF16),
            vm((2 * HL + 1, HD, HD), F32),
            vm((nz, 2 * HL + 1, rows, HD), F32),
            vm((ny, 2 * HL + 1, rows, HD), F32),
            vm((nz, 2 * HL, rows, HD), F32),
            vm((2 * HL, HD, HD), F32),
            vm((NJ, 2 * HL, HD, HD), F32),
            vm((NJ, 8, HD), F32),
            vm((NJ, 8, HD), F32),
            vm((NJ, HL, SPAN, SPAN), F32),
            vm((NJ, HL, SPAN, SPAN), F32),
            vm((NJ, HL, SPAN, 2 * HD), BF16),
            vm((NJ, HL, HD, 2 * SPAN), BF16),
            vm((NJ, HL, HD, 2 * SPAN), BF16),
            vm((NJ, HL, HD, SPAN), F32),
            vm((HL, HD, SPAN), F32),
            vm((HL, 3 * HD, 2 * HD), BF16),
            vm((HL, 3 * HD, 2 * HD), BF16),
            vm((HL, HD, SPAN), F32),
            vm((HL, HD, SPAN), F32),
            vm((HL, HD, SPAN), F32),
            vm((SPAN, HL * HD), BF16),
            vm((NJ, NCH, half, width), F32),
            vm((NJ, NCH, half, width), F32),
            vm((NJ, NCH, half, width), F32),
            vm((NCH // 2, half, width), F32),
            vm((NCH // 2, half, width), F32),
            vm((NCH, half, width), F32),
            vm((NCH, half, width), F32),
            dma,
            dma((4, nz)),
            dma((4, nz)),
            dma((2, ny)),
            dma((2, ny)),
            dma((NJ, NCH)),
            dma((NJ, NCH)),
            dma((NCH,)),
            dma((NCH,)),
            dma((2, NCH)),
            dma((2, NCH)),
        ]
        space = pl.BlockSpec(memory_space=pltpu.VMEM)
        return pl.pallas_call(
            functools.partial(kernel, ny, nz, nx),
            out_shape=jax.ShapeDtypeStruct((queries.shape[0] // (2 * nx), columns), BF16),
            in_specs=[space] * 5 + [pl.BlockSpec(memory_space=pl.ANY)],
            out_specs=space,
            scratch_shapes=scratch,
            compiler_params=pltpu.CompilerParams(
                collective_id=0, has_side_effects=True, vmem_limit_bytes=60 << 20
            ),
        )(queries, keys, values, log_decay, ridge[None, :], out_weight)

    placed = (
        P("seq", "wide"),
        P("seq", "wide"),
        P("seq", "wide"),
        P("seq", "wide"),
        P("wide"),
        P("wide", None),
    )
    return jax.shard_map(
        body, mesh=mesh, in_specs=placed, out_specs=P(("seq", "wide"), None), check_vma=False
    )
```

time: 373 us -> 97.5 us (0.26); the launches traced: 368 us -> 97.3 us
  waiting for transfers between devices: 160 us -> 0 us
  Pallas kernels: 0 us -> 93.9 us
  matrix products: 89.4 us -> 0 us
  blocking collectives: 65.5 us -> 0 us
  other arithmetic: 22.3 us -> 0 us
  between operations: 14.5 us -> 0.01 us
  local copies, waits for them, and re-layouts: 15.6 us -> 3.42 us
    all_gather x2 -> x0, waiting for transfers between devices: 107 us -> none  [the longest x1 85.5 us: body(): lax.all_gather(device_g[None], 'seq', axis=0, tiled=True)]
    pallas_call x0 -> x1, Pallas kernels: none -> 93.9 us  [body(): pl.pallas_call(functools.partial(kernel, ny, nz, nx), out_shape=jax.Shape...]
    dot_general x32 -> x0, matrix products: 89.4 us -> none  [the longest x8 19.5 us: span_read(): jnp.einsum('...ts,...sd->...td', operate_scores, key_rows, precision=high...]
    unnamed x1 -> x0, blocking collectives: 65.5 us -> none
    reduce_scatter x1 -> x0, waiting for transfers between devices: 52.4 us -> none  [body(): lax.psum_scatter(jnp.dot(normed, out_weight, preferred_element_type=jnp.f...]
    add x16 -> x0, other arithmetic: 7.1 us -> none  [the longest x4 4.29 us: combine_memories(): factor * earlier[1] + later[1]]
    reshape x5 -> x0, local copies, waits for them, and re-layouts: 6.46 us -> none  [the longest x4 5.75 us: unit_rows(): matrix.astype(jnp.float32).reshape(matrix.shape[0], head_count, head_size)]
    reduce_sum x9 -> x0, other arithmetic: 4.34 us -> none  [the longest x2 2.46 us: unit_rows(): jnp.sum(entries * entries, axis=-1, keepdims=True) + 1e-06]
  transfers between devices with their start and end apart: 3 -> 0, of which waited for: 3 -> 0; matrix products, arithmetic and copies ran while one was open for 7% -> 0% of each run, Pallas kernels for 0% -> 0%
where the time goes in v1:
time: 97.5 us; the launch traced here: 97.3 us
  Pallas kernels  93.9 us (96%)
  local copies, waits for them, and re-layouts  3.42 us (4%)
    pallas_call x1, Pallas kernels, body(): pl.pallas_call(functools.partial(kernel, ny, nz, nx), out_shape=jax.Shape...  93.9 us
    unnamed x2, local copies, waits for them, and re-layouts  3.42 us

profile of v1, /device:TPU:1, one launch (start us, length us, event | category | flops | bytes accessed | tf_op | source)
XLA Modules:
  0.0 97.3 jit_solution(16026465548915312357)
XLA Ops:
  0.0 1.5 %copy.7.ld_ref = f32[512,4]{1,0:T(8,128)} copy(f32[512,4]{0,1:T(4,128)} %param.9) | data formatting | bytes 16384 | tf_op args[3]
  1.6 93.9 %shard_map.64 = bf16[64,4096]{1,0:T(8,128)(2,1)} custom-call(bf16[512,512]{1,0:T(8,128)(2,1)} %q_ref.1, bf16[512,512]{1,0:T(8,128)(2,1)} %k_ref.1, bf16[512,512]{1,0:T(8,128)(2,1)} %v_ref.1, f32[512,4]{1,0:T(8,128)} %copy.7.ld_ref, f32[1,512]{1,0:T(1,128)} %bitcast.1, bf16[512,4096]{1,0:T(8,128)(2,1)} %w_hbm.1), custom_call_target="tpu_custom_call" | custom-call | tf_op jit(solution)/shard_map/pallas_call | solution.py:436
  95.4 1.9 %copy.9 = bf16[64,4096]{1,0:T(8,128)(2,1)} copy(bf16[64,4096]{1,0:T(8,128)(2,1)} %shard_map.64) | data formatting | bytes 1048576

commit v2 on v1

--- a/solution.py
+++ b/solution.py
@@ -13,6 +13,7 @@
 HD = 128
 SPAN = 128
 ITERS = 8
+UNROLL = 2
 HL = 4
 NJ = 4
 NCH = 8
@@ -206,8 +207,9 @@
     for h in range(HL):
         hc = slice(h * HD, (h + 1) * HD)
         ridge_m[h] = jnp.broadcast_to(ridge_ref[:, hc], (HD, HD)).T
-        a1[h, 2 * HD : 3 * HD, HD : 2 * HD] = jnp.zeros((HD, HD), BF16)
-        a2[h, 2 * HD : 3 * HD, HD : 2 * HD] = jnp.zeros((HD, HD), BF16)
+        for i in range(2):
+            a1[i * HL + h, 2 * HD : 3 * HD, HD : 2 * HD] = jnp.zeros((HD, HD), BF16)
+            a2[i * HL + h, 2 * HD : 3 * HD, HD : 2 * HD] = jnp.zeros((HD, HD), BF16)
 
     def weights_of(j):
         for h in range(HL):
@@ -233,55 +235,66 @@
     for copy in back:
         copy.wait_recv()
 
-    def system(ref, j, h, state):
+    def system(ref, slot, j, h, state):
         high, low = parts(state)
-        ref[h, 0:HD, :] = k2[j, h]
-        ref[h, HD : 2 * HD, 0:HD] = high
-        ref[h, HD : 2 * HD, HD : 2 * HD] = high
-        ref[h, 2 * HD : 3 * HD, 0:HD] = low
-
-    def solve(j):
+        ref[slot, 0:HD, :] = k2[j, h]
+        ref[slot, HD : 2 * HD, 0:HD] = high
+        ref[slot, HD : 2 * HD, HD : 2 * HD] = high
+        ref[slot, 2 * HD : 3 * HD, 0:HD] = low
+
+    def blocks_of(spans):
+        return [(i * HL + h, j, h) for i, j in enumerate(spans) for h in range(HL)]
+
+    def solve(spans):
+        blocks = blocks_of(spans)
         norm0, opening = [], []
-        for h in range(HL):
-            system(a1, j, h, sdec[j, h : h + 1, :] * pre[h] + lb[j, h])
+        for slot, j, h in blocks:
+            system(a1, slot, j, h, sdec[j, h : h + 1, :] * pre[h] + lb[j, h])
             query = qt[j, h]
-            xs[h] = jnp.zeros((HD, SPAN), F32)
-            rs[h] = query
-            ps[h] = query
+            xs[slot] = jnp.zeros((HD, SPAN), F32)
+            rs[slot] = query
+            ps[slot] = query
             norm0.append(jnp.sum(query * query, axis=0, keepdims=True))
             opening.append(jnp.exp(crow[j, h : h + 1, :]))
 
         def sweep(_, norm):
-            after = []
-            for h in range(HL):
-                direction = ps[h]
-                out = dot(a1[h], stacked(direction))
-                scores = out[0:HD] * w2[j, h]
-                image = (
-                    opening[h] * (out[HD : 2 * HD] + out[2 * HD : 3 * HD])
-                    + dot(kt2[j, h], stacked(scores))
-                    + ridge_m[h] * direction
-                )
-                alpha = norm[h] / jnp.sum(direction * image, axis=0, keepdims=True)
-                xs[h] = xs[h] + alpha * direction
-                residual = rs[h] - alpha * image
+            n = len(blocks)
+            outs, locals_, after = [None] * n, [None] * n, [None] * n
+            for i, (slot, j, h) in enumerate(blocks):
+                outs[i] = dot(a1[slot], stacked(ps[slot]))
+            for i, (slot, j, h) in enumerate(blocks):
+                locals_[i] = dot(kt2[j, h], stacked(outs[i][0:HD] * w2[j, h]))
+            for i, (slot, j, h) in enumerate(blocks):
+                direction = ps[slot]
+                carried = outs[i][HD : 2 * HD] + outs[i][2 * HD : 3 * HD]
+                image = opening[i] * carried + locals_[i] + ridge_m[h] * direction
+                alpha = norm[i] / jnp.sum(direction * image, axis=0, keepdims=True)
+                xs[slot] = xs[slot] + alpha * direction
+                residual = rs[slot] - alpha * image
                 fresh = jnp.sum(residual * residual, axis=0, keepdims=True)
-                rs[h] = residual
-                ps[h] = residual + (fresh / norm[h]) * direction
-                after.append(fresh)
+                rs[slot] = residual
+                ps[slot] = residual + (fresh / norm[i]) * direction
+                after[i] = fresh
             return tuple(after)
 
-        lax.fori_loop(0, ITERS, sweep, tuple(norm0))
+        lax.fori_loop(0, ITERS, sweep, tuple(norm0), unroll=UNROLL)
         return opening
 
-    def finish(j, opening):
-        for h in range(HL):
-            system(a2, j, h, sdec[j, h : h + 1, :] * pre[HL + h] + lb[j, HL + h])
-            out = dot(a2[h], stacked(xs[h]))
-            scores = out[0:HD] * w1[j, h]
-            read = opening[h] * (out[HD : 2 * HD] + out[2 * HD : 3 * HD]) + dot(vt2[j, h], stacked(scores))
+    def finish(k, i, j, opening):
+        outs = []
+        for h in range(HL):
+            slot = i * HL + h
+            system(a2, slot, j, h, sdec[j, h : h + 1, :] * pre[HL + h] + lb[j, HL + h])
+        for h in range(HL):
+            slot = i * HL + h
+            outs.append(dot(a2[slot], stacked(xs[slot])))
+        reads = []
+        for h in range(HL):
+            reads.append(dot(vt2[j, h], stacked(outs[h][0:HD] * w1[j, h])))
+        for h in range(HL):
+            read = opening[i * HL + h] * (outs[h][HD : 2 * HD] + outs[h][2 * HD : 3 * HD]) + reads[h]
             read = read * lax.rsqrt(jnp.sum(read * read, axis=0, keepdims=True) * (1.0 / HD) + 1e-06)
-            nm[:, h * HD : (h + 1) * HD] = read.T.astype(BF16)
+            nm[k, :, h * HD : (h + 1) * HD] = read.T.astype(BF16)
 
     half = SPAN // 2
     width = w_vm.shape[1] // NCH
@@ -295,7 +308,7 @@
     def project(k, first):
         mine = pl.multiple_of(c * half, half)
         other = pl.multiple_of((1 - c) * half, half)
-        lhs = jnp.concatenate([nm[pl.ds(mine, half), :], nm[pl.ds(other, half), :]], axis=0)
+        lhs = jnp.concatenate([nm[k, pl.ds(mine, half), :], nm[k, pl.ds(other, half), :]], axis=0)
         copies = {}
         for i in range(NCH):
             n = (first + i) % NCH
@@ -317,10 +330,10 @@
     middle = NCH // 2
     js = [lax.rem(x + o, nx) for o in ORDER]
 
-    opening = solve(js[0])
+    opening = solve(js[0:1])
     for copy in g_back:
         copy.wait_recv()
-    finish(js[0], opening)
+    finish(0, 0, js[0], opening)
     load_w.wait()
     copies = project(0, 0)
     relay = {}
@@ -335,17 +348,16 @@
     sent += list(copies.values()) + list(relay.values())
 
     final1, final2 = {}, {}
-    opening = solve(js[1])
-    finish(js[1], opening)
+    opening = solve(js[1:3])
+    finish(1, 0, js[1], opening)
     copies1 = project(1, middle)
-    for n in range(middle, NCH):
-        copies1[n].wait_recv()
-        pown[1, n] = pown[1, n] + pin[1, n]
-        final1[n] = x_copy(pown.at[1, n], f1.at[n], f_send.at[0, n], f_recv.at[0, n], right)
-    opening = solve(js[2])
-    finish(js[2], opening)
+    finish(2, 1, js[2], opening)
     copies2 = project(2, 0)
     for n in range(middle):
+        m = n + middle
+        copies1[m].wait_recv()
+        pown[1, m] = pown[1, m] + pin[1, m]
+        final1[m] = x_copy(pown.at[1, m], f1.at[m], f_send.at[0, m], f_recv.at[0, m], right)
         copies2[n].wait_recv()
         pown[2, n] = pown[2, n] + pin[2, n]
         final2[n] = x_copy(pown.at[2, n], f2.at[n], f_send.at[1, n], f_recv.at[1, n], left)
@@ -361,8 +373,8 @@
         final2[m] = x_copy(pown.at[2, m], f2.at[m], f_send.at[1, m], f_recv.at[1, m], left)
     sent += list(copies1.values()) + list(copies2.values()) + list(final1.values()) + list(final2.values())
 
-    opening = solve(js[3])
-    finish(js[3], opening)
+    opening = solve(js[3:4])
+    finish(3, 0, js[3], opening)
     copies3 = project(3, 0)
     sent += list(copies3.values())
     for n in range(NCH):
@@ -407,12 +419,12 @@
             vm((NJ, HL, HD, 2 * SPAN), BF16),
             vm((NJ, HL, HD, SPAN), F32),
             vm((HL, HD, SPAN), F32),
-            vm((HL, 3 * HD, 2 * HD), BF16),
-            vm((HL, 3 * HD, 2 * HD), BF16),
-            vm((HL, HD, SPAN), F32),
-            vm((HL, HD, SPAN), F32),
-            vm((HL, HD, SPAN), F32),
-            vm((SPAN, HL * HD), BF16),
+            vm((2 * HL, 3 * HD, 2 * HD), BF16),
+            vm((2 * HL, 3 * HD, 2 * HD), BF16),
+            vm((2 * HL, HD, SPAN), F32),
+            vm((2 * HL, HD, SPAN), F32),
+            vm((2 * HL, HD, SPAN), F32),
+            vm((NJ, SPAN, HL * HD), BF16),
             vm((NJ, NCH, half, width), F32),
             vm((NJ, NCH, half, width), F32),
             vm((NJ, NCH, half, width), F32),

time: 97.5 us -> 87.7 us (0.90)
  Pallas kernels: 93.9 us -> 84 us
    pallas_call x1, Pallas kernels: 93.9 us -> 84 us  [body(): pl.pallas_call(functools.partial(kernel, ny, nz, nx), out_shape=jax.Shape...]
where the time goes in v2:
time: 87.7 us; the launch traced here: 87.5 us
  Pallas kernels  84 us (96%)
  local copies, waits for them, and re-layouts  3.42 us (4%)
    pallas_call x1, Pallas kernels, body(): pl.pallas_call(functools.partial(kernel, ny, nz, nx), out_shape=jax.Shape...  84 us
    unnamed x2, local copies, waits for them, and re-layouts  3.42 us

profile of v2, /device:TPU:1, one launch (start us, length us, event | category | flops | bytes accessed | tf_op | source)
XLA Modules:
  0.0 87.5 jit_solution(10338521545670919732)
XLA Ops:
  0.0 1.5 %copy.7.ld_ref = f32[512,4]{1,0:T(8,128)} copy(f32[512,4]{0,1:T(4,128)} %param.9) | data formatting | bytes 16384 | tf_op args[3]
  1.6 84.0 %shard_map.64 = bf16[64,4096]{1,0:T(8,128)(2,1)} custom-call(bf16[512,512]{1,0:T(8,128)(2,1)} %q_ref.1, bf16[512,512]{1,0:T(8,128)(2,1)} %k_ref.1, bf16[512,512]{1,0:T(8,128)(2,1)} %v_ref.1, f32[512,4]{1,0:T(8,128)} %copy.7.ld_ref, f32[1,512]{1,0:T(1,128)} %bitcast.1, bf16[512,4096]{1,0:T(8,128)(2,1)} %w_hbm.1), custom_call_target="tpu_custom_call" | custom-call | tf_op jit(solution)/shard_map/pallas_call | solution.py:448
  85.6 1.9 %copy.9 = bf16[64,4096]{1,0:T(8,128)(2,1)} copy(bf16[64,4096]{1,0:T(8,128)(2,1)} %shard_map.64) | data formatting | bytes 1048576

commit v3 on v2

--- a/solution.py
+++ b/solution.py
@@ -36,22 +36,32 @@
 
 def kernel(
     ny, nz, nx,
-    q_ref, k_ref, v_ref, ld_ref, ridge_ref, w_hbm, o_ref,
-    w_vm, st, buf1, tot, buf2, pre, lb, sdec, crow, w1, w2, k2, kt2, vt2, qt, ridge_m,
-    a1, a2, xs, rs, ps, nm, pown, pout, pin, ra, rb, f1, f2,
-    w_sem, z_send, z_recv, y_send, y_recv, p_send, p_recv, r_send, r_recv, f_send, f_recv,
+    q_hbm, k_hbm, v_hbm, ld_hbm, ridge_hbm, w_hbm, o_ref,
+    q_ref, k_ref, v_ref, ld_ref, ridge_ref, w_vm,
+    st_h, st_g, buf_h, buf_g, tot_h, tot_g, out_h, out_g, pre_h, pre, lb, sdec, crow, w1, w2, k2, kt2, vt2, qt, ridge_m,
+    gram_in, a1, a2, xs, rs, ps, nm, pown, pout, pin, ra, rb, f1, f2,
+    load_sem, z_send, z_recv, y_send, y_recv, p_send, p_recv, r_send, r_recv, f_send, f_recv,
 ):
     seq = lax.axis_index("seq")
     wide = lax.axis_index("wide")
     y, z = lax.div(seq, nz), lax.rem(seq, nz)
     x, c = lax.div(wide, 2), lax.rem(wide, 2)
-    rows = HD // nz
+    rows_h, rows_g = HD // 2 // nz, HD // nz
     partner = x * 2 + (1 - c)
     right = lax.rem(x + 1, nx) * 2 + c
     left = lax.rem(x + nx - 1, nx) * 2 + c
 
-    load_w = pltpu.make_async_copy(w_hbm, w_vm, w_sem)
-    load_w.start()
+    loads = [
+        pltpu.make_async_copy(src, dst, load_sem.at[i])
+        for i, (src, dst) in enumerate(
+            (
+                (ld_hbm, ld_ref), (k_hbm, k_ref), (v_hbm, v_ref),
+                (q_hbm, q_ref), (ridge_hbm, ridge_ref), (w_hbm, w_vm),
+            )
+        )
+    ]
+    for load in loads[:5]:
+        load.start()
 
     barrier = pltpu.get_barrier_semaphore()
     for step in range(1, nz):
@@ -68,25 +78,26 @@
     lower = (place_r >= place_c).astype(F32)
     upper = (place_r <= place_c).astype(F32)
     ccols, norms = [], {}
+    loads[0].wait()
     total = jnp.zeros((1, HL), F32)
     closings = []
     for j in range(NJ):
-        decay = ld_ref[j * SPAN : (j + 1) * SPAN, :]
-        ccol = jnp.dot(lower, decay, precision=highest, preferred_element_type=F32)
+        decay = ld_ref[:, j * SPAN : (j + 1) * SPAN]
+        ccol = lax.dot_general(
+            lower, decay, (((1,), (1,)), ((), ())), precision=highest, preferred_element_type=F32
+        )
         ccols.append(ccol)
-        crow[j, 0:HL, :] = lax.dot_general(
-            decay, upper, (((0,), (0,)), ((), ())), precision=highest, preferred_element_type=F32
-        )
+        crow[j, 0:HL, :] = jnp.dot(decay, upper, precision=highest, preferred_element_type=F32)
         for h in range(HL):
             sdec[j, h : h + 1, :] = jnp.exp(jnp.broadcast_to(total[:, h : h + 1], (1, HD)))
         closing = ccol[SPAN - 1 : SPAN, :]
         closings.append(closing)
         total = total + closing
-    group = lax.rem(place_r, rows)
-    marks = jnp.zeros((HD, HD), F32)
-    for h in range(HL):
-        marks = jnp.where(group == h, jnp.broadcast_to(total[:, h : h + 1], (HD, HD)), marks)
-    st[0] = marks
+    group = lax.rem(lax.broadcasted_iota(jnp.int32, (HD // 2, HD), 0), rows_h)
+    near = lax.rem(place_c - place_r + HD, HD)
+    keep = near[0 : HD // 2] < HD // 2
+    marks = jnp.zeros((HD // 2, HD), F32)
+    loads[1].wait()
 
     for h in range(HL):
         hc = slice(h * HD, (h + 1) * HD)
@@ -105,7 +116,11 @@
             gram = dot(kt2[j, h], stacked(keyf * (fade * norm * norm)))
             lb[j, h] = run
             run = jnp.exp(closings[j][:, h : h + 1]) * run + gram
-        st[1 + h] = run
+        st_h[1 + h] = jnp.where(keep, run[0 : HD // 2], run[HD // 2 :])
+        edge = jnp.sum(jnp.where(near == HD // 2, run, 0.0), axis=0, keepdims=True)
+        marks = jnp.where(group == h, jnp.broadcast_to(total[:, h : h + 1], marks.shape), marks)
+        marks = jnp.where(group == HL + h, edge, marks)
+    st_h[0] = marks
 
     pl.semaphore_wait(barrier, nz + ny + 1)
 
@@ -116,22 +131,20 @@
             device_id=(to, wide), device_id_type=MESH,
         )
 
-    bands = ((0, HL + 1), (HL + 1, 2 * HL + 1))
-
-    def scatter(band):
-        lo, hi = bands[band]
+    def scatter(st, buf, slot, rows):
         copies = []
         for step in range(1, nz):
             peer = lax.rem(z + step, nz)
             start = pl.multiple_of(peer * rows, rows)
-            copies.append(z_copy(st.at[lo:hi, pl.ds(start, rows), :], buf1.at[z, lo:hi], band, step))
+            copies.append(z_copy(st.at[:, pl.ds(start, rows), :], buf.at[z], slot, step))
             copies[-1].start()
         mine = pl.multiple_of(z * rows, rows)
-        buf1[z, lo:hi] = st[lo:hi, pl.ds(mine, rows), :]
+        buf[z] = st[:, pl.ds(mine, rows), :]
         return copies
 
-    sends = scatter(0)
+    sends = scatter(st_h, buf_h, 0, rows_h)
     sent = list(sends)
+    loads[2].wait()
 
     for h in range(HL):
         hc = slice(h * HD, (h + 1) * HD)
@@ -145,65 +158,106 @@
             memory = dot(vt2[j, h], stacked(keyf * (fade * norms[j, h])))
             lb[j, HL + h] = run
             run = jnp.exp(closings[j][:, h : h + 1]) * run + memory
-        st[1 + HL + h] = run
-    g_sends = scatter(1)
-    sent += g_sends
-
-    def row_total(band, copies):
-        for copy in copies:
-            copy.wait_recv()
-        lo, hi = bands[band]
-        first = 1 + band * HL
-        sums = [jnp.zeros((rows, HD), F32) for _ in range(HL)]
-        decay = jnp.zeros((8, HD), F32)
-        for other in range(nz):
-            marks = buf1[other, 0, 0:8, :]
-            factor = jnp.exp(marks)
-            decay = decay + marks
-            for h in range(HL):
-                sums[h] = factor[h : h + 1] * sums[h] + buf1[other, first + h]
-        for h in range(HL):
-            tot[y, first + h] = sums[h]
-        if band == 0:
-            tot[y, 0] = jnp.zeros((rows, HD), F32)
-            tot[y, 0, 0:8, :] = decay
+        st_g[h] = run
+    g_sends = scatter(st_g, buf_g, 1, rows_g)
+
+    def y_copies(buf, slot):
         copies = []
         for step in range(1, ny):
             to = lax.rem(y + step, ny) * nz + z
             copies.append(
                 pltpu.make_async_remote_copy(
-                    src_ref=tot.at[y, lo:hi], dst_ref=tot.at[y, lo:hi],
-                    send_sem=y_send.at[band, step], recv_sem=y_recv.at[band, step],
+                    src_ref=buf.at[y], dst_ref=buf.at[y],
+                    send_sem=y_send.at[slot, step], recv_sem=y_recv.at[slot, step],
                     device_id=(to, wide), device_id_type=MESH,
                 )
             )
             copies[-1].start()
         return copies
 
-    def give_back(band, copies):
-        for copy in copies:
-            copy.wait_recv()
-        first = 1 + band * HL
-        runs = [jnp.zeros((rows, HD), F32) for _ in range(HL)]
-        for other in range(ny):
-            factor = jnp.exp(tot[other, 0, 0:8, :])
-            for h in range(HL):
-                runs[h] = jnp.where(other < y, factor[h : h + 1] * runs[h] + tot[other, first + h], runs[h])
-        for other in range(nz):
-            factor = jnp.exp(buf1[other, 0, 0:8, :])
-            for h in range(HL):
-                buf2[other, band * HL + h] = runs[h]
-                runs[h] = factor[h : h + 1] * runs[h] + buf1[other, first + h]
-        lo, hi = band * HL, (band + 1) * HL
+    def give_back(buf, pre, slot, rows):
         mine = pl.multiple_of(z * rows, rows)
         copies = []
         for step in range(1, nz):
             peer = lax.rem(z + step, nz)
-            copies.append(z_copy(buf2.at[peer, lo:hi], pre.at[lo:hi, pl.ds(mine, rows), :], 2 + band, step))
+            copies.append(z_copy(buf.at[peer], pre.at[:, pl.ds(mine, rows), :], slot, step))
             copies[-1].start()
-        pre[lo:hi, pl.ds(mine, rows), :] = buf2[z, lo:hi]
+        pre[:, pl.ds(mine, rows), :] = buf[z]
         return copies
 
+    def total_h(copies):
+        for copy in copies:
+            copy.wait_recv()
+        sums = [jnp.zeros((rows_h, HD), F32) for _ in range(HL)]
+        edges = [jnp.zeros((1, HD), F32) for _ in range(HL)]
+        decay = jnp.zeros((8, HD), F32)
+        for other in range(nz):
+            marks = buf_h[other, 0, 0:8, :]
+            factor = jnp.exp(marks[0:HL])
+            decay = decay + marks
+            for h in range(HL):
+                sums[h] = factor[h : h + 1] * sums[h] + buf_h[other, 1 + h]
+                edges[h] = factor[h : h + 1] * edges[h] + marks[HL + h : HL + h + 1]
+        tot_h[y, 0, 0:8, :] = decay
+        for h in range(HL):
+            tot_h[y, 1 + h] = sums[h]
+            tot_h[y, 0, HL + h : HL + h + 1, :] = edges[h]
+        return y_copies(tot_h, 0)
+
+    def prefix_h(copies):
+        for copy in copies:
+            copy.wait_recv()
+        runs = [jnp.zeros((rows_h, HD), F32) for _ in range(HL)]
+        edges = [jnp.zeros((1, HD), F32) for _ in range(HL)]
+        for other in range(ny):
+            marks = tot_h[other, 0, 0:8, :]
+            factor = jnp.exp(marks[0:HL])
+            for h in range(HL):
+                runs[h] = jnp.where(other < y, factor[h : h + 1] * runs[h] + tot_h[other, 1 + h], runs[h])
+                edges[h] = jnp.where(
+                    other < y, factor[h : h + 1] * edges[h] + marks[HL + h : HL + h + 1], edges[h]
+                )
+        for other in range(nz):
+            marks = buf_h[other, 0, 0:8, :]
+            factor = jnp.exp(marks[0:HL])
+            for h in range(HL):
+                out_h[other, 1 + h] = runs[h]
+                out_h[other, 0, HL + h : HL + h + 1, :] = edges[h]
+                runs[h] = factor[h : h + 1] * runs[h] + buf_h[other, 1 + h]
+                edges[h] = factor[h : h + 1] * edges[h] + marks[HL + h : HL + h + 1]
+        return give_back(out_h, pre_h, 2, rows_h)
+
+    def total_g(copies):
+        for copy in copies:
+            copy.wait_recv()
+        sums = [jnp.zeros((rows_g, HD), F32) for _ in range(HL)]
+        for other in range(nz):
+            factor = jnp.exp(buf_h[other, 0, 0:HL, :])
+            for h in range(HL):
+                sums[h] = factor[h : h + 1] * sums[h] + buf_g[other, h]
+        for h in range(HL):
+            tot_g[y, h] = sums[h]
+        return y_copies(tot_g, 1)
+
+    def prefix_g(copies):
+        for copy in copies:
+            copy.wait_recv()
+        runs = [jnp.zeros((rows_g, HD), F32) for _ in range(HL)]
+        for other in range(ny):
+            factor = jnp.exp(tot_h[other, 0, 0:HL, :])
+            for h in range(HL):
+                runs[h] = jnp.where(other < y, factor[h : h + 1] * runs[h] + tot_g[other, h], runs[h])
+        for other in range(nz):
+            factor = jnp.exp(buf_h[other, 0, 0:HL, :])
+            for h in range(HL):
+                out_g[other, h] = runs[h]
+                runs[h] = factor[h : h + 1] * runs[h] + buf_g[other, h]
+        return give_back(out_g, pre, 3, rows_g)
+
+    loads[3].wait()
+    loads[4].wait()
+    loads[5].start()
+    out_h[:, 0] = jnp.zeros((nz, rows_h, HD), F32)
     for h in range(HL):
         hc = slice(h * HD, (h + 1) * HD)
         ridge_m[h] = jnp.broadcast_to(ridge_ref[:, hc], (HD, HD)).T
@@ -224,16 +278,23 @@
 
     weights_of(0)
     weights_of(1)
-    y_sends = row_total(0, sends)
+    y_sends = total_h(sends)
+    sent += y_sends
     weights_of(2)
-    back = give_back(0, y_sends)
-    sent += y_sends + back
-    y_sends = row_total(1, g_sends)
+    back = prefix_h(y_sends)
+    sent += back
     weights_of(3)
-    g_back = give_back(1, y_sends)
-    sent += y_sends + g_back
+    y_sends = total_g(g_sends)
+    sent += y_sends + g_sends
+    g_back = prefix_g(y_sends)
+    sent += g_back
     for copy in back:
         copy.wait_recv()
+    for h in range(HL):
+        packed = pre_h[1 + h]
+        spread = jnp.concatenate([jnp.where(keep, packed, 0.0), jnp.where(keep, 0.0, packed)], axis=0)
+        both = jnp.where(near == 0, spread, spread + spread.T)
+        gram_in[h] = jnp.where(near == HD // 2, pre_h[0, HL + h : HL + h + 1, :], both)
 
     def system(ref, slot, j, h, state):
         high, low = parts(state)
@@ -249,7 +310,7 @@
         blocks = blocks_of(spans)
         norm0, opening = [], []
         for slot, j, h in blocks:
-            system(a1, slot, j, h, sdec[j, h : h + 1, :] * pre[h] + lb[j, h])
+            system(a1, slot, j, h, sdec[j, h : h + 1, :] * gram_in[h] + lb[j, h])
             query = qt[j, h]
             xs[slot] = jnp.zeros((HD, SPAN), F32)
             rs[slot] = query
@@ -284,7 +345,7 @@
         outs = []
         for h in range(HL):
             slot = i * HL + h
-            system(a2, slot, j, h, sdec[j, h : h + 1, :] * pre[HL + h] + lb[j, HL + h])
+            system(a2, slot, j, h, sdec[j, h : h + 1, :] * pre[h] + lb[j, HL + h])
         for h in range(HL):
             slot = i * HL + h
             outs.append(dot(a2[slot], stacked(xs[slot])))
@@ -334,7 +395,7 @@
     for copy in g_back:
         copy.wait_recv()
     finish(0, 0, js[0], opening)
-    load_w.wait()
+    loads[5].wait()
     copies = project(0, 0)
     relay = {}
     for i in range(NCH):
@@ -399,16 +460,27 @@
         columns = out_weight.shape[1]
         width = columns // NCH
         half = SPAN // 2
-        rows = HD // nz
+        rows_h, rows_g = HD // 2 // nz, HD // nz
+        tokens, inner = queries.shape
         vm = pltpu.VMEM
         dma = pltpu.SemaphoreType.DMA
         scratch = [
+            vm((tokens, inner), BF16),
+            vm((tokens, inner), BF16),
+            vm((tokens, inner), BF16),
+            vm((HL, tokens), F32),
+            vm((1, inner), F32),
             vm(out_weight.shape, BF16),
-            vm((2 * HL + 1, HD, HD), F32),
-            vm((nz, 2 * HL + 1, rows, HD), F32),
-            vm((ny, 2 * HL + 1, rows, HD), F32),
-            vm((nz, 2 * HL, rows, HD), F32),
-            vm((2 * HL, HD, HD), F32),
+            vm((HL + 1, HD // 2, HD), F32),
+            vm((HL, HD, HD), F32),
+            vm((nz, HL + 1, rows_h, HD), F32),
+            vm((nz, HL, rows_g, HD), F32),
+            vm((ny, HL + 1, rows_h, HD), F32),
+            vm((ny, HL, rows_g, HD), F32),
+            vm((nz, HL + 1, rows_h, HD), F32),
+            vm((nz, HL, rows_g, HD), F32),
+            vm((HL + 1, HD // 2, HD), F32),
+            vm((HL, HD, HD), F32),
             vm((NJ, 2 * HL, HD, HD), F32),
             vm((NJ, 8, HD), F32),
             vm((NJ, 8, HD), F32),
@@ -419,6 +491,7 @@
             vm((NJ, HL, HD, 2 * SPAN), BF16),
             vm((NJ, HL, HD, SPAN), F32),
             vm((HL, HD, SPAN), F32),
+            vm((HL, HD, HD), F32),
             vm((2 * HL, 3 * HD, 2 * HD), BF16),
             vm((2 * HL, 3 * HD, 2 * HD), BF16),
             vm((2 * HL, HD, SPAN), F32),
@@ -432,7 +505,7 @@
             vm((NCH // 2, half, width), F32),
             vm((NCH, half, width), F32),
             vm((NCH, half, width), F32),
-            dma,
+            dma((6,)),
             dma((4, nz)),
             dma((4, nz)),
             dma((2, ny)),
@@ -448,13 +521,13 @@
         return pl.pallas_call(
             functools.partial(kernel, ny, nz, nx),
             out_shape=jax.ShapeDtypeStruct((queries.shape[0] // (2 * nx), columns), BF16),
-            in_specs=[space] * 5 + [pl.BlockSpec(memory_space=pl.ANY)],
+            in_specs=[pl.BlockSpec(memory_space=pl.ANY)] * 6,
             out_specs=space,
             scratch_shapes=scratch,
             compiler_params=pltpu.CompilerParams(
                 collective_id=0, has_side_effects=True, vmem_limit_bytes=60 << 20
             ),
-        )(queries, keys, values, log_decay, ridge[None, :], out_weight)
+        )(queries, keys, values, log_decay.T, ridge[None, :], out_weight)
 
     placed = (
         P("seq", "wide"),

time: 87.7 us -> 80.1 us (0.913)
  Pallas kernels: 84 us -> 78 us
  local copies, waits for them, and re-layouts: 3.42 us -> 1.87 us
    pallas_call x1, Pallas kernels: 84 us -> 78 us  [body(): pl.pallas_call(functools.partial(kernel, ny, nz, nx), out_shape=jax.Shape...]
    unnamed x2 -> x1, local copies, waits for them, and re-layouts: 3.42 us -> 1.87 us
where the time goes in v3:
time: 80.1 us; the launch traced here: 79.9 us
  Pallas kernels  78 us (97%)
  local copies, waits for them, and re-layouts  1.87 us (2%)
    pallas_call x1, Pallas kernels, body(): pl.pallas_call(functools.partial(kernel, ny, nz, nx), out_shape=jax.Shape...  78 us
    unnamed x1, local copies, waits for them, and re-layouts  1.87 us

profile of v3, /device:TPU:1, one launch (start us, length us, event | category | flops | bytes accessed | tf_op | source)
XLA Modules:
  0.0 79.9 jit_solution(12671795770243716298)
XLA Ops:
  0.0 78.0 %shard_map.64 = bf16[64,4096]{1,0:T(8,128)(2,1)} custom-call(bf16[512,512]{1,0:T(8,128)(2,1)} %q_hbm.1, bf16[512,512]{1,0:T(8,128)(2,1)} %k_hbm.1, bf16[512,512]{1,0:T(8,128)(2,1)} %v_hbm.1, f32[4,512]{1,0:T(4,128)} %bitcast.2, f32[1,512]{1,0:T(1,128)} %bitcast.3, bf16[512,4096]{1,0:T(8,128)(2,1)} %w_hbm.1), custom_call_target="tpu_custom_call" | custom-call | tf_op jit(solution)/shard_map/pallas_call | solution.py:521
  78.1 1.9 %copy.8 = bf16[64,4096]{1,0:T(8,128)(2,1)} copy(bf16[64,4096]{1,0:T(8,128)(2,1)} %shard_map.64) | data formatting | bytes 1048576

commit v4 on v3

--- a/solution.py
+++ b/solution.py
@@ -14,6 +14,7 @@
 SPAN = 128
 ITERS = 8
 UNROLL = 2
+LAG = 4
 HL = 4
 NJ = 4
 NCH = 8
@@ -38,8 +39,8 @@
     ny, nz, nx,
     q_hbm, k_hbm, v_hbm, ld_hbm, ridge_hbm, w_hbm, o_ref,
     q_ref, k_ref, v_ref, ld_ref, ridge_ref, w_vm,
-    st_h, st_g, buf_h, buf_g, tot_h, tot_g, out_h, out_g, pre_h, pre, lb, sdec, crow, w1, w2, k2, kt2, vt2, qt, ridge_m,
-    gram_in, a1, a2, xs, rs, ps, nm, pown, pout, pin, ra, rb, f1, f2,
+    st_h, st_g, buf_h, buf_g, tot_h, tot_g, out_h, out_g, pre_h, pre, lb, sdec, crow, w1, w2, kt2, vt2, qt, ridge_m,
+    gram_in, g_in, a1, a2, xs, rs, ps, nm, pown, pout, pin, ra, rb, f1, f2,
     load_sem, z_send, z_recv, y_send, y_recv, p_send, p_recv, r_send, r_recv, f_send, f_recv,
 ):
     seq = lax.axis_index("seq")
@@ -104,8 +105,8 @@
         run = jnp.zeros((HD, HD), F32)
         for j in range(NJ):
             keys = k_ref[j * SPAN : (j + 1) * SPAN, hc]
-            k2[j, h, :, 0:HD] = keys
-            k2[j, h, :, HD : 2 * HD] = keys
+            a2[j, h, 0:HD, 0:HD] = keys
+            a2[j, h, 0:HD, HD : 2 * HD] = keys
             keyf = keys.astype(F32)
             norm = lax.rsqrt(jnp.sum(keyf * keyf, axis=1, keepdims=True) + 1e-06)
             norms[j, h] = norm
@@ -131,19 +132,20 @@
             device_id=(to, wide), device_id_type=MESH,
         )
 
-    def scatter(st, buf, slot, rows):
+    def scatter(st, buf, slot, rows, part):
         copies = []
         for step in range(1, nz):
             peer = lax.rem(z + step, nz)
             start = pl.multiple_of(peer * rows, rows)
-            copies.append(z_copy(st.at[:, pl.ds(start, rows), :], buf.at[z], slot, step))
+            copies.append(z_copy(st.at[part, pl.ds(start, rows), :], buf.at[z, part], slot, step))
             copies[-1].start()
         mine = pl.multiple_of(z * rows, rows)
-        buf[z] = st[:, pl.ds(mine, rows), :]
+        buf[z, part] = st[part, pl.ds(mine, rows), :]
         return copies
 
-    sends = scatter(st_h, buf_h, 0, rows_h)
+    sends = scatter(st_h, buf_h, 0, rows_h, slice(0, HL + 1))
     sent = list(sends)
+    g_sends = []
     loads[2].wait()
 
     for h in range(HL):
@@ -159,15 +161,16 @@
             lb[j, HL + h] = run
             run = jnp.exp(closings[j][:, h : h + 1]) * run + memory
         st_g[h] = run
-    g_sends = scatter(st_g, buf_g, 1, rows_g)
-
-    def y_copies(buf, slot):
+        g_sends.append(scatter(st_g, buf_g, 1 + h, rows_g, h))
+        sent += g_sends[h]
+
+    def y_copies(buf, slot, part):
         copies = []
         for step in range(1, ny):
             to = lax.rem(y + step, ny) * nz + z
             copies.append(
                 pltpu.make_async_remote_copy(
-                    src_ref=buf.at[y], dst_ref=buf.at[y],
+                    src_ref=buf.at[y, part], dst_ref=buf.at[y, part],
                     send_sem=y_send.at[slot, step], recv_sem=y_recv.at[slot, step],
                     device_id=(to, wide), device_id_type=MESH,
                 )
@@ -175,14 +178,16 @@
             copies[-1].start()
         return copies
 
-    def give_back(buf, pre, slot, rows):
+    def give_back(buf, pre, slot, rows, part):
         mine = pl.multiple_of(z * rows, rows)
         copies = []
         for step in range(1, nz):
             peer = lax.rem(z + step, nz)
-            copies.append(z_copy(buf.at[peer], pre.at[:, pl.ds(mine, rows), :], slot, step))
+            copies.append(
+                z_copy(buf.at[peer, part], pre.at[part, pl.ds(mine, rows), :], slot, step)
+            )
             copies[-1].start()
-        pre[:, pl.ds(mine, rows), :] = buf[z]
+        pre[part, pl.ds(mine, rows), :] = buf[z, part]
         return copies
 
     def total_h(copies):
@@ -202,7 +207,7 @@
         for h in range(HL):
             tot_h[y, 1 + h] = sums[h]
             tot_h[y, 0, HL + h : HL + h + 1, :] = edges[h]
-        return y_copies(tot_h, 0)
+        return y_copies(tot_h, 0, slice(0, HL + 1))
 
     def prefix_h(copies):
         for copy in copies:
@@ -225,34 +230,28 @@
                 out_h[other, 0, HL + h : HL + h + 1, :] = edges[h]
                 runs[h] = factor[h : h + 1] * runs[h] + buf_h[other, 1 + h]
                 edges[h] = factor[h : h + 1] * edges[h] + marks[HL + h : HL + h + 1]
-        return give_back(out_h, pre_h, 2, rows_h)
-
-    def total_g(copies):
+        return give_back(out_h, pre_h, 1 + HL, rows_h, slice(0, HL + 1))
+
+    def total_g(h, copies):
         for copy in copies:
             copy.wait_recv()
-        sums = [jnp.zeros((rows_g, HD), F32) for _ in range(HL)]
+        run = jnp.zeros((rows_g, HD), F32)
         for other in range(nz):
-            factor = jnp.exp(buf_h[other, 0, 0:HL, :])
-            for h in range(HL):
-                sums[h] = factor[h : h + 1] * sums[h] + buf_g[other, h]
-        for h in range(HL):
-            tot_g[y, h] = sums[h]
-        return y_copies(tot_g, 1)
-
-    def prefix_g(copies):
+            run = jnp.exp(buf_h[other, 0, h : h + 1, :]) * run + buf_g[other, h]
+        tot_g[y, h] = run
+        return y_copies(tot_g, 1 + h, h)
+
+    def prefix_g(h, copies):
         for copy in copies:
             copy.wait_recv()
-        runs = [jnp.zeros((rows_g, HD), F32) for _ in range(HL)]
+        run = jnp.zeros((rows_g, HD), F32)
         for other in range(ny):
-            factor = jnp.exp(tot_h[other, 0, 0:HL, :])
-            for h in range(HL):
-                runs[h] = jnp.where(other < y, factor[h : h + 1] * runs[h] + tot_g[other, h], runs[h])
+            factor = jnp.exp(tot_h[other, 0, h : h + 1, :])
+            run = jnp.where(other < y, factor * run + tot_g[other, h], run)
         for other in range(nz):
-            factor = jnp.exp(buf_h[other, 0, 0:HL, :])
-            for h in range(HL):
-                out_g[other, h] = runs[h]
-                runs[h] = factor[h : h + 1] * runs[h] + buf_g[other, h]
-        return give_back(out_g, pre, 3, rows_g)
+            out_g[other, h] = run
+            run = jnp.exp(buf_h[other, 0, h : h + 1, :]) * run + buf_g[other, h]
+        return give_back(out_g, pre, 2 + HL + h, rows_g, h)
 
     loads[3].wait()
     loads[4].wait()
@@ -261,9 +260,9 @@
     for h in range(HL):
         hc = slice(h * HD, (h + 1) * HD)
         ridge_m[h] = jnp.broadcast_to(ridge_ref[:, hc], (HD, HD)).T
+        g_in[h, HD : 2 * HD, HD : 2 * HD] = jnp.zeros((HD, HD), BF16)
         for i in range(2):
             a1[i * HL + h, 2 * HD : 3 * HD, HD : 2 * HD] = jnp.zeros((HD, HD), BF16)
-            a2[i * HL + h, 2 * HD : 3 * HD, HD : 2 * HD] = jnp.zeros((HD, HD), BF16)
 
     def weights_of(j):
         for h in range(HL):
@@ -271,6 +270,11 @@
             lag = crow[j, h : h + 1, :] - ccols[j][:, h : h + 1]
             causal = place_r <= place_c
             weight = jnp.where(causal, jnp.exp(jnp.where(causal, lag, 0.0)), 0.0) * norms[j, h]
+            high, low = parts(lb[j, HL + h])
+            a2[j, h, HD : 2 * HD, 0:HD] = high
+            a2[j, h, HD : 2 * HD, HD : 2 * HD] = high
+            a2[j, h, 2 * HD : 3 * HD, 0:HD] = low
+            a2[j, h, 2 * HD : 3 * HD, HD : 2 * HD] = jnp.zeros((HD, HD), BF16)
             w1[j, h] = weight
             w2[j, h] = weight * norms[j, h]
             query = q_ref[j * SPAN : (j + 1) * SPAN, hc].astype(F32).T
@@ -284,10 +288,10 @@
     back = prefix_h(y_sends)
     sent += back
     weights_of(3)
-    y_sends = total_g(g_sends)
-    sent += y_sends + g_sends
-    g_back = prefix_g(y_sends)
-    sent += g_back
+    gy_sends = [total_g(h, g_sends[h]) for h in range(HL)]
+    g_back = [prefix_g(h, gy_sends[h]) for h in range(HL)]
+    for h in range(HL):
+        sent += gy_sends[h] + g_back[h]
     for copy in back:
         copy.wait_recv()
     for h in range(HL):
@@ -296,12 +300,12 @@
         both = jnp.where(near == 0, spread, spread + spread.T)
         gram_in[h] = jnp.where(near == HD // 2, pre_h[0, HL + h : HL + h + 1, :], both)
 
-    def system(ref, slot, j, h, state):
+    def system(slot, j, h, state):
         high, low = parts(state)
-        ref[slot, 0:HD, :] = k2[j, h]
-        ref[slot, HD : 2 * HD, 0:HD] = high
-        ref[slot, HD : 2 * HD, HD : 2 * HD] = high
-        ref[slot, 2 * HD : 3 * HD, 0:HD] = low
+        a1[slot, 0:HD, :] = a2[j, h, 0:HD, :]
+        a1[slot, HD : 2 * HD, 0:HD] = high
+        a1[slot, HD : 2 * HD, HD : 2 * HD] = high
+        a1[slot, 2 * HD : 3 * HD, 0:HD] = low
 
     def blocks_of(spans):
         return [(i * HL + h, j, h) for i, j in enumerate(spans) for h in range(HL)]
@@ -310,7 +314,7 @@
         blocks = blocks_of(spans)
         norm0, opening = [], []
         for slot, j, h in blocks:
-            system(a1, slot, j, h, sdec[j, h : h + 1, :] * gram_in[h] + lb[j, h])
+            system(slot, j, h, sdec[j, h : h + 1, :] * gram_in[h] + lb[j, h])
             query = qt[j, h]
             xs[slot] = jnp.zeros((HD, SPAN), F32)
             rs[slot] = query
@@ -341,19 +345,23 @@
         lax.fori_loop(0, ITERS, sweep, tuple(norm0), unroll=UNROLL)
         return opening
 
-    def finish(k, i, j, opening):
-        outs = []
+    def read_local(i, j, opening):
+        outs = [dot(a2[j, h], stacked(xs[i * HL + h])) for h in range(HL)]
         for h in range(HL):
-            slot = i * HL + h
-            system(a2, slot, j, h, sdec[j, h : h + 1, :] * pre[h] + lb[j, HL + h])
-        for h in range(HL):
-            slot = i * HL + h
-            outs.append(dot(a2[slot], stacked(xs[slot])))
-        reads = []
-        for h in range(HL):
-            reads.append(dot(vt2[j, h], stacked(outs[h][0:HD] * w1[j, h])))
-        for h in range(HL):
-            read = opening[i * HL + h] * (outs[h][HD : 2 * HD] + outs[h][2 * HD : 3 * HD]) + reads[h]
+            near_part = dot(vt2[j, h], stacked(outs[h][0:HD] * w1[j, h]))
+            rs[i * HL + h] = near_part + opening[i * HL + h] * (outs[h][HD : 2 * HD] + outs[h][2 * HD :])
+
+    def take_memory(h):
+        high, low = parts(pre[h])
+        g_in[h, 0:HD, 0:HD] = high
+        g_in[h, 0:HD, HD : 2 * HD] = high
+        g_in[h, HD : 2 * HD, 0:HD] = low
+
+    def read_out(k, i, j, opening, heads):
+        outs = [dot(g_in[h], stacked(xs[i * HL + h])) for h in heads]
+        for h, out in zip(heads, outs):
+            lifted = opening[i * HL + h] * sdec[j, h : h + 1, :]
+            read = rs[i * HL + h] + lifted * (out[0:HD] + out[HD : 2 * HD])
             read = read * lax.rsqrt(jnp.sum(read * read, axis=0, keepdims=True) * (1.0 / HD) + 1e-06)
             nm[k, :, h * HD : (h + 1) * HD] = read.T.astype(BF16)
 
@@ -366,19 +374,26 @@
             device_id=(seq, partner), device_id_type=MESH,
         )
 
-    def project(k, first):
+    def project(k, order, use):
         mine = pl.multiple_of(c * half, half)
         other = pl.multiple_of((1 - c) * half, half)
         lhs = jnp.concatenate([nm[k, pl.ds(mine, half), :], nm[k, pl.ds(other, half), :]], axis=0)
         copies = {}
-        for i in range(NCH):
-            n = (first + i) % NCH
-            out = dot(lhs, w_vm[:, n * width : (n + 1) * width])
-            pown[k, n] = out[0:half]
-            pout[k, n] = out[half:]
-            copies[n] = p_copy(k, n)
-            copies[n].start()
+        for i in range(NCH + LAG):
+            if i < NCH:
+                n = order[i]
+                out = dot(lhs, w_vm[:, n * width : (n + 1) * width])
+                pown[k, n] = out[0:half]
+                pout[k, n] = out[half:]
+                copies[n] = p_copy(k, n)
+                copies[n].start()
+            if i >= LAG:
+                use(order[i - LAG], copies)
         return copies
+
+    def join(k, n, copies):
+        copies[n].wait_recv()
+        pown[k, n] = pown[k, n] + pin[k, n]
 
     def x_copy(src, dst, send, recv, to):
         copy = pltpu.make_async_remote_copy(
@@ -391,56 +406,63 @@
     middle = NCH // 2
     js = [lax.rem(x + o, nx) for o in ORDER]
 
+    mixed_order = [(i % 2) * middle + i // 2 for i in range(NCH)]
+    relay, final1, final2 = {}, {}, {}
+
     opening = solve(js[0:1])
-    for copy in g_back:
-        copy.wait_recv()
-    finish(0, 0, js[0], opening)
+    read_local(0, js[0], opening)
     loads[5].wait()
-    copies = project(0, 0)
-    relay = {}
-    for i in range(NCH):
-        n = (i % 2) * middle + i // 2
-        copies[n].wait_recv()
-        pown[0, n] = pown[0, n] + pin[0, n]
+    for h in range(HL):
+        for copy in g_back[h]:
+            copy.wait_recv()
+        take_memory(h)
+        read_out(0, 0, js[0], opening, (h,))
+
+    def send_relay(n, copies):
+        join(0, n, copies)
         if n < middle:
             relay[n] = x_copy(pown.at[0, n], ra.at[n], r_send.at[n], r_recv.at[n], right)
         else:
             relay[n] = x_copy(pown.at[0, n], rb.at[n - middle], r_send.at[n], r_recv.at[n], left)
+
+    copies = project(0, mixed_order, send_relay)
     sent += list(copies.values()) + list(relay.values())
 
-    final1, final2 = {}, {}
+    def send_right(n, copies):
+        if n >= middle:
+            join(1, n, copies)
+            final1[n] = x_copy(pown.at[1, n], f1.at[n], f_send.at[0, n], f_recv.at[0, n], right)
+
+    def send_left(n, copies):
+        if n < middle:
+            join(2, n, copies)
+            final2[n] = x_copy(pown.at[2, n], f2.at[n], f_send.at[1, n], f_recv.at[1, n], left)
+
     opening = solve(js[1:3])
-    finish(1, 0, js[1], opening)
-    copies1 = project(1, middle)
-    finish(2, 1, js[2], opening)
-    copies2 = project(2, 0)
+    every = tuple(range(HL))
+    read_local(0, js[1], opening)
+    read_out(1, 0, js[1], opening, every)
+    copies1 = project(1, list(range(middle, NCH)) + list(range(middle)), send_right)
+    read_local(1, js[2], opening)
+    read_out(2, 1, js[2], opening, every)
+    copies2 = project(2, list(range(NCH)), send_left)
     for n in range(middle):
-        m = n + middle
-        copies1[m].wait_recv()
-        pown[1, m] = pown[1, m] + pin[1, m]
-        final1[m] = x_copy(pown.at[1, m], f1.at[m], f_send.at[0, m], f_recv.at[0, m], right)
-        copies2[n].wait_recv()
-        pown[2, n] = pown[2, n] + pin[2, n]
-        final2[n] = x_copy(pown.at[2, n], f2.at[n], f_send.at[1, n], f_recv.at[1, n], left)
-    for n in range(middle):
-        copies1[n].wait_recv()
         relay[n].wait_recv()
-        pown[1, n] = pown[1, n] + pin[1, n] + ra[n]
+        join(1, n, copies1)
+        pown[1, n] = pown[1, n] + ra[n]
         final1[n] = x_copy(pown.at[1, n], f1.at[n], f_send.at[0, n], f_recv.at[0, n], right)
         m = n + middle
-        copies2[m].wait_recv()
         relay[m].wait_recv()
-        pown[2, m] = pown[2, m] + pin[2, m] + rb[n]
+        join(2, m, copies2)
+        pown[2, m] = pown[2, m] + rb[n]
         final2[m] = x_copy(pown.at[2, m], f2.at[m], f_send.at[1, m], f_recv.at[1, m], left)
     sent += list(copies1.values()) + list(copies2.values()) + list(final1.values()) + list(final2.values())
 
     opening = solve(js[3:4])
-    finish(3, 0, js[3], opening)
-    copies3 = project(3, 0)
+    read_local(0, js[3], opening)
+    read_out(3, 0, js[3], opening, every)
+    copies3 = project(3, list(range(NCH)), functools.partial(join, 3))
     sent += list(copies3.values())
-    for n in range(NCH):
-        copies3[n].wait_recv()
-        pown[3, n] = pown[3, n] + pin[3, n]
     for i in range(NCH):
         n = (i % 2) * middle + i // 2
         m = (n + middle) % NCH
@@ -486,14 +508,14 @@
             vm((NJ, 8, HD), F32),
             vm((NJ, HL, SPAN, SPAN), F32),
             vm((NJ, HL, SPAN, SPAN), F32),
-            vm((NJ, HL, SPAN, 2 * HD), BF16),
             vm((NJ, HL, HD, 2 * SPAN), BF16),
             vm((NJ, HL, HD, 2 * SPAN), BF16),
             vm((NJ, HL, HD, SPAN), F32),
             vm((HL, HD, SPAN), F32),
             vm((HL, HD, HD), F32),
+            vm((HL, 2 * HD, 2 * HD), BF16),
             vm((2 * HL, 3 * HD, 2 * HD), BF16),
-            vm((2 * HL, 3 * HD, 2 * HD), BF16),
+            vm((NJ, HL, 3 * HD, 2 * HD), BF16),
             vm((2 * HL, HD, SPAN), F32),
             vm((2 * HL, HD, SPAN), F32),
             vm((2 * HL, HD, SPAN), F32),
@@ -506,10 +528,10 @@
             vm((NCH, half, width), F32),
             vm((NCH, half, width), F32),
             dma((6,)),
-            dma((4, nz)),
-            dma((4, nz)),
-            dma((2, ny)),
-            dma((2, ny)),
+            dma((2 * HL + 2, nz)),
+            dma((2 * HL + 2, nz)),
+            dma((HL + 1, ny)),
+            dma((HL + 1, ny)),
             dma((NJ, NCH)),
             dma((NJ, NCH)),
             dma((NCH,)),

time: 80.1 us -> 80.5 us (level)
  no operation moved by 1% of the time
where the time goes in v4:
time: 80.5 us; the launch traced here: 80.4 us
  Pallas kernels  78.5 us (98%)
  local copies, waits for them, and re-layouts  1.87 us (2%)
    pallas_call x1, Pallas kernels, body(): pl.pallas_call(functools.partial(kernel, ny, nz, nx), out_shape=jax.Shape...  78.5 us
    unnamed x1, local copies, waits for them, and re-layouts  1.87 us

profile of v4, /device:TPU:1, one launch (start us, length us, event | category | flops | bytes accessed | tf_op | source)
XLA Modules:
  0.0 80.4 jit_solution(9403576453425764464)
XLA Ops:
  0.0 78.5 %shard_map.64 = bf16[64,4096]{1,0:T(8,128)(2,1)} custom-call(bf16[512,512]{1,0:T(8,128)(2,1)} %q_hbm.1, bf16[512,512]{1,0:T(8,128)(2,1)} %k_hbm.1, bf16[512,512]{1,0:T(8,128)(2,1)} %v_hbm.1, f32[4,512]{1,0:T(4,128)} %bitcast.2, f32[1,512]{1,0:T(1,128)} %bitcast.3, bf16[512,4096]{1,0:T(8,128)(2,1)} %w_hbm.1), custom_call_target="tpu_custom_call" | custom-call | tf_op jit(solution)/shard_map/pallas_call | solution.py:543
  78.5 1.9 %copy.8 = bf16[64,4096]{1,0:T(8,128)(2,1)} copy(bf16[64,4096]{1,0:T(8,128)(2,1)} %shard_map.64) | data formatting | bytes 1048576

commit v5 on v4

--- a/solution.py
+++ b/solution.py
@@ -13,8 +13,10 @@
 HD = 128
 SPAN = 128
 ITERS = 8
-UNROLL = 2
+UNROLL = 3
+FULL = 6
 LAG = 4
+PAIR = 2
 HL = 4
 NJ = 4
 NCH = 8
@@ -40,7 +42,7 @@
     q_hbm, k_hbm, v_hbm, ld_hbm, ridge_hbm, w_hbm, o_ref,
     q_ref, k_ref, v_ref, ld_ref, ridge_ref, w_vm,
     st_h, st_g, buf_h, buf_g, tot_h, tot_g, out_h, out_g, pre_h, pre, lb, sdec, crow, w1, w2, kt2, vt2, qt, ridge_m,
-    gram_in, g_in, a1, a2, xs, rs, ps, nm, pown, pout, pin, ra, rb, f1, f2,
+    gram_in, g_in, a1, b1, a2, xs, rs, ps, nm, pown, pout, pin, ra, rb, f1, f2,
     load_sem, z_send, z_recv, y_send, y_recv, p_send, p_recv, r_send, r_recv, f_send, f_recv,
 ):
     seq = lax.axis_index("seq")
@@ -161,8 +163,9 @@
             lb[j, HL + h] = run
             run = jnp.exp(closings[j][:, h : h + 1]) * run + memory
         st_g[h] = run
-        g_sends.append(scatter(st_g, buf_g, 1 + h, rows_g, h))
-        sent += g_sends[h]
+        if h % PAIR == PAIR - 1:
+            g_sends.append(scatter(st_g, buf_g, 1 + h, rows_g, slice(h + 1 - PAIR, h + 1)))
+            sent += g_sends[-1]
 
     def y_copies(buf, slot, part):
         copies = []
@@ -222,41 +225,43 @@
                 edges[h] = jnp.where(
                     other < y, factor[h : h + 1] * edges[h] + marks[HL + h : HL + h + 1], edges[h]
                 )
+        mine = list(edges)
         for other in range(nz):
             marks = buf_h[other, 0, 0:8, :]
             factor = jnp.exp(marks[0:HL])
             for h in range(HL):
-                out_h[other, 1 + h] = runs[h]
-                out_h[other, 0, HL + h : HL + h + 1, :] = edges[h]
+                out_h[other, h] = runs[h]
+                mine[h] = jnp.where(other == z, edges[h], mine[h])
                 runs[h] = factor[h : h + 1] * runs[h] + buf_h[other, 1 + h]
                 edges[h] = factor[h : h + 1] * edges[h] + marks[HL + h : HL + h + 1]
-        return give_back(out_h, pre_h, 1 + HL, rows_h, slice(0, HL + 1))
-
-    def total_g(h, copies):
+        return give_back(out_h, pre_h, 1 + HL, rows_h, slice(0, HL)), mine
+
+    def total_g(first, copies):
         for copy in copies:
             copy.wait_recv()
-        run = jnp.zeros((rows_g, HD), F32)
-        for other in range(nz):
-            run = jnp.exp(buf_h[other, 0, h : h + 1, :]) * run + buf_g[other, h]
-        tot_g[y, h] = run
-        return y_copies(tot_g, 1 + h, h)
-
-    def prefix_g(h, copies):
+        for h in range(first, first + PAIR):
+            run = jnp.zeros((rows_g, HD), F32)
+            for other in range(nz):
+                run = jnp.exp(buf_h[other, 0, h : h + 1, :]) * run + buf_g[other, h]
+            tot_g[y, h] = run
+        return y_copies(tot_g, 1 + first, slice(first, first + PAIR))
+
+    def prefix_g(first, copies):
         for copy in copies:
             copy.wait_recv()
-        run = jnp.zeros((rows_g, HD), F32)
-        for other in range(ny):
-            factor = jnp.exp(tot_h[other, 0, h : h + 1, :])
-            run = jnp.where(other < y, factor * run + tot_g[other, h], run)
-        for other in range(nz):
-            out_g[other, h] = run
-            run = jnp.exp(buf_h[other, 0, h : h + 1, :]) * run + buf_g[other, h]
-        return give_back(out_g, pre, 2 + HL + h, rows_g, h)
+        for h in range(first, first + PAIR):
+            run = jnp.zeros((rows_g, HD), F32)
+            for other in range(ny):
+                factor = jnp.exp(tot_h[other, 0, h : h + 1, :])
+                run = jnp.where(other < y, factor * run + tot_g[other, h], run)
+            for other in range(nz):
+                out_g[other, h] = run
+                run = jnp.exp(buf_h[other, 0, h : h + 1, :]) * run + buf_g[other, h]
+        return give_back(out_g, pre, 2 + HL + first, rows_g, slice(first, first + PAIR))
 
     loads[3].wait()
     loads[4].wait()
     loads[5].start()
-    out_h[:, 0] = jnp.zeros((nz, rows_h, HD), F32)
     for h in range(HL):
         hc = slice(h * HD, (h + 1) * HD)
         ridge_m[h] = jnp.broadcast_to(ridge_ref[:, hc], (HD, HD)).T
@@ -285,20 +290,21 @@
     y_sends = total_h(sends)
     sent += y_sends
     weights_of(2)
-    back = prefix_h(y_sends)
+    back, edges = prefix_h(y_sends)
     sent += back
     weights_of(3)
-    gy_sends = [total_g(h, g_sends[h]) for h in range(HL)]
-    g_back = [prefix_g(h, gy_sends[h]) for h in range(HL)]
-    for h in range(HL):
-        sent += gy_sends[h] + g_back[h]
+    firsts = range(0, HL, PAIR)
+    gy_sends = [total_g(first, copies) for first, copies in zip(firsts, g_sends)]
+    g_back = [prefix_g(first, copies) for first, copies in zip(firsts, gy_sends)]
+    for copies in gy_sends + g_back:
+        sent += copies
     for copy in back:
         copy.wait_recv()
     for h in range(HL):
-        packed = pre_h[1 + h]
+        packed = pre_h[h]
         spread = jnp.concatenate([jnp.where(keep, packed, 0.0), jnp.where(keep, 0.0, packed)], axis=0)
         both = jnp.where(near == 0, spread, spread + spread.T)
-        gram_in[h] = jnp.where(near == HD // 2, pre_h[0, HL + h : HL + h + 1, :], both)
+        gram_in[h] = jnp.where(near == HD // 2, edges[h], both)
 
     def system(slot, j, h, state):
         high, low = parts(state)
@@ -306,6 +312,8 @@
         a1[slot, HD : 2 * HD, 0:HD] = high
         a1[slot, HD : 2 * HD, HD : 2 * HD] = high
         a1[slot, 2 * HD : 3 * HD, 0:HD] = low
+        b1[slot, :, 0:HD] = high
+        b1[slot, :, HD : 2 * HD] = kt2[j, h, :, 0:SPAN]
 
     def blocks_of(spans):
         return [(i * HL + h, j, h) for i, j in enumerate(spans) for h in range(HL)]
@@ -322,6 +330,16 @@
             norm0.append(jnp.sum(query * query, axis=0, keepdims=True))
             opening.append(jnp.exp(crow[j, h : h + 1, :]))
 
+        def advance(i, slot, norm, image):
+            direction = ps[slot]
+            alpha = norm / jnp.sum(direction * image, axis=0, keepdims=True)
+            xs[slot] = xs[slot] + alpha * direction
+            residual = rs[slot] - alpha * image
+            fresh = jnp.sum(residual * residual, axis=0, keepdims=True)
+            rs[slot] = residual
+            ps[slot] = residual + (fresh / norm) * direction
+            return fresh
+
         def sweep(_, norm):
             n = len(blocks)
             outs, locals_, after = [None] * n, [None] * n, [None] * n
@@ -330,19 +348,27 @@
             for i, (slot, j, h) in enumerate(blocks):
                 locals_[i] = dot(kt2[j, h], stacked(outs[i][0:HD] * w2[j, h]))
             for i, (slot, j, h) in enumerate(blocks):
-                direction = ps[slot]
                 carried = outs[i][HD : 2 * HD] + outs[i][2 * HD : 3 * HD]
-                image = opening[i] * carried + locals_[i] + ridge_m[h] * direction
-                alpha = norm[i] / jnp.sum(direction * image, axis=0, keepdims=True)
-                xs[slot] = xs[slot] + alpha * direction
-                residual = rs[slot] - alpha * image
-                fresh = jnp.sum(residual * residual, axis=0, keepdims=True)
-                rs[slot] = residual
-                ps[slot] = residual + (fresh / norm[i]) * direction
-                after[i] = fresh
+                image = opening[i] * carried + locals_[i] + ridge_m[h] * ps[slot]
+                after[i] = advance(i, slot, norm[i], image)
             return tuple(after)
 
-        lax.fori_loop(0, ITERS, sweep, tuple(norm0), unroll=UNROLL)
+        def last_sweep(_, norm):
+            n = len(blocks)
+            outs, images, after = [None] * n, [None] * n, [None] * n
+            for i, (slot, j, h) in enumerate(blocks):
+                outs[i] = dot(a1[slot, 0:HD, 0:HD], ps[slot].astype(BF16))
+            for i, (slot, j, h) in enumerate(blocks):
+                lifted = (opening[i] * ps[slot]).astype(BF16)
+                scores = (outs[i] * w2[j, h]).astype(BF16)
+                images[i] = dot(b1[slot], jnp.concatenate([lifted, scores], axis=0))
+            for i, (slot, j, h) in enumerate(blocks):
+                image = images[i] + ridge_m[h] * ps[slot]
+                after[i] = advance(i, slot, norm[i], image)
+            return tuple(after)
+
+        norm = lax.fori_loop(0, FULL, sweep, tuple(norm0), unroll=UNROLL)
+        lax.fori_loop(FULL, ITERS, last_sweep, norm, unroll=2)
         return opening
 
     def read_local(i, j, opening):
@@ -412,11 +438,12 @@
     opening = solve(js[0:1])
     read_local(0, js[0], opening)
     loads[5].wait()
-    for h in range(HL):
-        for copy in g_back[h]:
+    for first, copies in zip(firsts, g_back):
+        for copy in copies:
             copy.wait_recv()
-        take_memory(h)
-        read_out(0, 0, js[0], opening, (h,))
+        for h in range(first, first + PAIR):
+            take_memory(h)
+        read_out(0, 0, js[0], opening, tuple(range(first, first + PAIR)))
 
     def send_relay(n, copies):
         join(0, n, copies)
@@ -499,9 +526,9 @@
             vm((nz, HL, rows_g, HD), F32),
             vm((ny, HL + 1, rows_h, HD), F32),
             vm((ny, HL, rows_g, HD), F32),
-            vm((nz, HL + 1, rows_h, HD), F32),
+            vm((nz, HL, rows_h, HD), F32),
             vm((nz, HL, rows_g, HD), F32),
-            vm((HL + 1, HD // 2, HD), F32),
+            vm((HL, HD // 2, HD), F32),
             vm((HL, HD, HD), F32),
             vm((NJ, 2 * HL, HD, HD), F32),
             vm((NJ, 8, HD), F32),
@@ -515,6 +542,7 @@
             vm((HL, HD, HD), F32),
             vm((HL, 2 * HD, 2 * HD), BF16),
             vm((2 * HL, 3 * HD, 2 * HD), BF16),
+            vm((2 * HL, HD, 2 * HD), BF16),
             vm((NJ, HL, 3 * HD, 2 * HD), BF16),
             vm((2 * HL, HD, SPAN), F32),
             vm((2 * HL, HD, SPAN), F32),

time: 80.5 us -> 78.4 us (0.974)
  Pallas kernels: 78.5 us -> 76.4 us
    pallas_call x1, Pallas kernels: 78.5 us -> 76.4 us  [body(): pl.pallas_call(functools.partial(kernel, ny, nz, nx), out_shape=jax.Shape...]
where the time goes in v5:
time: 78.4 us; the launch traced here: 78.3 us
  Pallas kernels  76.4 us (97%)
  local copies, waits for them, and re-layouts  1.87 us (2%)
    pallas_call x1, Pallas kernels, body(): pl.pallas_call(functools.partial(kernel, ny, nz, nx), out_shape=jax.Shape...  76.4 us
    unnamed x1, local copies, waits for them, and re-layouts  1.87 us

profile of v5, /device:TPU:1, one launch (start us, length us, event | category | flops | bytes accessed | tf_op | source)
XLA Modules:
  0.0 78.3 jit_solution(9703418679876202140)
XLA Ops:
  0.0 76.4 %shard_map.64 = bf16[64,4096]{1,0:T(8,128)(2,1)} custom-call(bf16[512,512]{1,0:T(8,128)(2,1)} %q_hbm.1, bf16[512,512]{1,0:T(8,128)(2,1)} %k_hbm.1, bf16[512,512]{1,0:T(8,128)(2,1)} %v_hbm.1, f32[4,512]{1,0:T(4,128)} %bitcast.2, f32[1,512]{1,0:T(1,128)} %bitcast.3, bf16[512,4096]{1,0:T(8,128)(2,1)} %w_hbm.1), custom_call_target="tpu_custom_call" | custom-call | tf_op jit(solution)/shard_map/pallas_call | solution.py:571
  76.4 1.9 %copy.8 = bf16[64,4096]{1,0:T(8,128)(2,1)} copy(bf16[64,4096]{1,0:T(8,128)(2,1)} %shard_map.64) | data formatting | bytes 1048576

commit v6 on v5

--- a/solution.py
+++ b/solution.py
@@ -483,13 +483,15 @@
         join(2, m, copies2)
         pown[2, m] = pown[2, m] + rb[n]
         final2[m] = x_copy(pown.at[2, m], f2.at[m], f_send.at[1, m], f_recv.at[1, m], left)
-    sent += list(copies1.values()) + list(copies2.values()) + list(final1.values()) + list(final2.values())
+    sent += list(copies1.values()) + list(copies2.values())
 
     opening = solve(js[3:4])
     read_local(0, js[3], opening)
     read_out(3, 0, js[3], opening, every)
     copies3 = project(3, list(range(NCH)), functools.partial(join, 3))
     sent += list(copies3.values())
+    for copy in sent:
+        copy.wait_send()
     for i in range(NCH):
         n = (i % 2) * middle + i // 2
         m = (n + middle) % NCH
@@ -498,7 +500,7 @@
         if i % 2 == 1:
             for e in (n, m):
                 o_ref[:, e * width : (e + 1) * width] = (pown[3, e] + f1[e] + f2[e]).astype(BF16)
-    for copy in sent:
+    for copy in list(final1.values()) + list(final2.values()):
         copy.wait_send()
 
 

time: 78.4 us -> 78.3 us (level)
  no operation moved by 1% of the time
where the time goes in v6:
time: 78.3 us; the launch traced here: 78.2 us
  Pallas kernels  76.3 us (97%)
  local copies, waits for them, and re-layouts  1.87 us (2%)
    pallas_call x1, Pallas kernels, body(): pl.pallas_call(functools.partial(kernel, ny, nz, nx), out_shape=jax.Shape...  76.3 us
    unnamed x1, local copies, waits for them, and re-layouts  1.87 us

profile of v6, /device:TPU:1, one launch (start us, length us, event | category | flops | bytes accessed | tf_op | source)
XLA Modules:
  0.0 78.2 jit_solution(3787065818018555065)
XLA Ops:
  0.0 76.3 %shard_map.64 = bf16[64,4096]{1,0:T(8,128)(2,1)} custom-call(bf16[512,512]{1,0:T(8,128)(2,1)} %q_hbm.1, bf16[512,512]{1,0:T(8,128)(2,1)} %k_hbm.1, bf16[512,512]{1,0:T(8,128)(2,1)} %v_hbm.1, f32[4,512]{1,0:T(4,128)} %bitcast.2, f32[1,512]{1,0:T(1,128)} %bitcast.3, bf16[512,4096]{1,0:T(8,128)(2,1)} %w_hbm.1), custom_call_target="tpu_custom_call" | custom-call | tf_op jit(solution)/shard_map/pallas_call | solution.py:573
  76.3 1.9 %copy.8 = bf16[64,4096]{1,0:T(8,128)(2,1)} copy(bf16[64,4096]{1,0:T(8,128)(2,1)} %shard_map.64) | data formatting | bytes 1048576

commit v7 on v6

--- a/solution.py
+++ b/solution.py
@@ -577,9 +577,9 @@
             out_specs=space,
             scratch_shapes=scratch,
             compiler_params=pltpu.CompilerParams(
-                collective_id=0, has_side_effects=True, vmem_limit_bytes=60 << 20
+                collective_id=0, has_side_effects=True, vmem_limit_bytes=50000 << 10
             ),
-        )(queries, keys, values, log_decay.T, ridge[None, :], out_weight)
+        )(*(pltpu.with_memory_space_constraint(a, pltpu.HBM) for a in (queries, keys, values, log_decay.T, ridge[None, :], out_weight)))
 
     placed = (
         P("seq", "wide"),

time: 78.3 us -> 76.4 us (0.976)
  local copies, waits for them, and re-layouts: 1.87 us -> 0.8 us
  Pallas kernels: 76.3 us -> 75.5 us
    unnamed x1, local copies, waits for them, and re-layouts: 1.87 us -> 0.8 us
    pallas_call x1, Pallas kernels: 76.3 us -> 75.5 us  [body(): pl.pallas_call(functools.partial(kernel, ny, nz, nx), out_shape=jax.Shape...]
where the time goes in v7:
time: 76.4 us; the launch traced here: 76.3 us
  Pallas kernels  75.5 us (99%)
  local copies, waits for them, and re-layouts  0.8 us (1%)
    pallas_call x1, Pallas kernels, body(): pl.pallas_call(functools.partial(kernel, ny, nz, nx), out_shape=jax.Shape...  75.5 us

profile of v7, /device:TPU:1, one launch (start us, length us, event | category | flops | bytes accessed | tf_op | source)
XLA Modules:
  0.0 76.3 jit_solution(8088148944741325273)
XLA Ops:
  0.0 75.5 %shard_map.64 = bf16[64,4096]{1,0:T(8,128)(2,1)S(1)} custom-call(bf16[512,512]{1,0:T(8,128)(2,1)} %q_hbm.1, bf16[512,512]{1,0:T(8,128)(2,1)} %k_hbm.1, bf16[512,512]{1,0:T(8,128)(2,1)} %v_hbm.1, f32[4,512]{1,0:T(4,128)} %bitcast.2, f32[1,512]{1,0:T(1,128)} %bitcast.3, bf16[512,4096]{1,0:T(8,128)(2,1)} %w_hbm.1), custom_call_target="tpu_custom_call" | custom-call | tf_op jit(solution)/shard_map/pallas_call | solution.py:573
  75.5 0.8 %copy.8 = bf16[64,4096]{1,0:T(8,128)(2,1)} copy(bf16[64,4096]{1,0:T(8,128)(2,1)S(1)} %shard_map.64) | data formatting | bytes 1048576

commit v8 on v7

--- a/solution.py
+++ b/solution.py
@@ -400,25 +400,28 @@
             device_id=(seq, partner), device_id_type=MESH,
         )
 
-    def project(k, order, use):
+    def project(items, use):
         mine = pl.multiple_of(c * half, half)
         other = pl.multiple_of((1 - c) * half, half)
-        lhs = jnp.concatenate([nm[k, pl.ds(mine, half), :], nm[k, pl.ds(other, half), :]], axis=0)
+        lhs = {
+            k: jnp.concatenate([nm[k, pl.ds(mine, half), :], nm[k, pl.ds(other, half), :]], axis=0)
+            for k in dict(items)
+        }
         copies = {}
-        for i in range(NCH + LAG):
-            if i < NCH:
-                n = order[i]
-                out = dot(lhs, w_vm[:, n * width : (n + 1) * width])
+        for i in range(len(items) + LAG):
+            if i < len(items):
+                k, n = items[i]
+                out = dot(lhs[k], w_vm[:, n * width : (n + 1) * width])
                 pown[k, n] = out[0:half]
                 pout[k, n] = out[half:]
-                copies[n] = p_copy(k, n)
-                copies[n].start()
+                copies[k, n] = p_copy(k, n)
+                copies[k, n].start()
             if i >= LAG:
-                use(order[i - LAG], copies)
+                use(*items[i - LAG], copies)
         return copies
 
     def join(k, n, copies):
-        copies[n].wait_recv()
+        copies[k, n].wait_recv()
         pown[k, n] = pown[k, n] + pin[k, n]
 
     def x_copy(src, dst, send, recv, to):
@@ -445,51 +448,47 @@
             take_memory(h)
         read_out(0, 0, js[0], opening, tuple(range(first, first + PAIR)))
 
-    def send_relay(n, copies):
-        join(0, n, copies)
+    def send_relay(k, n, copies):
+        join(k, n, copies)
         if n < middle:
             relay[n] = x_copy(pown.at[0, n], ra.at[n], r_send.at[n], r_recv.at[n], right)
         else:
             relay[n] = x_copy(pown.at[0, n], rb.at[n - middle], r_send.at[n], r_recv.at[n], left)
 
-    copies = project(0, mixed_order, send_relay)
+    copies = project([(0, n) for n in mixed_order], send_relay)
     sent += list(copies.values()) + list(relay.values())
 
-    def send_right(n, copies):
-        if n >= middle:
-            join(1, n, copies)
+    def send_first(k, n, copies):
+        if k == 1 and n >= middle:
+            join(k, n, copies)
             final1[n] = x_copy(pown.at[1, n], f1.at[n], f_send.at[0, n], f_recv.at[0, n], right)
-
-    def send_left(n, copies):
-        if n < middle:
-            join(2, n, copies)
+        if k == 2 and n < middle:
+            join(k, n, copies)
             final2[n] = x_copy(pown.at[2, n], f2.at[n], f_send.at[1, n], f_recv.at[1, n], left)
 
     opening = solve(js[1:3])
     every = tuple(range(HL))
-    read_local(0, js[1], opening)
-    read_out(1, 0, js[1], opening, every)
-    copies1 = project(1, list(range(middle, NCH)) + list(range(middle)), send_right)
-    read_local(1, js[2], opening)
-    read_out(2, 1, js[2], opening, every)
-    copies2 = project(2, list(range(NCH)), send_left)
+    for i in range(2):
+        read_local(i, js[1 + i], opening)
+        read_out(1 + i, i, js[1 + i], opening, every)
+    pairs = [(k, (n + middle * (k % 2)) % NCH) for n in range(NCH) for k in (1, 2)]
+    copies = project(pairs, send_first)
+    sent += list(copies.values())
     for n in range(middle):
         relay[n].wait_recv()
-        join(1, n, copies1)
+        join(1, n, copies)
         pown[1, n] = pown[1, n] + ra[n]
         final1[n] = x_copy(pown.at[1, n], f1.at[n], f_send.at[0, n], f_recv.at[0, n], right)
         m = n + middle
         relay[m].wait_recv()
-        join(2, m, copies2)
+        join(2, m, copies)
         pown[2, m] = pown[2, m] + rb[n]
         final2[m] = x_copy(pown.at[2, m], f2.at[m], f_send.at[1, m], f_recv.at[1, m], left)
-    sent += list(copies1.values()) + list(copies2.values())
 
     opening = solve(js[3:4])
     read_local(0, js[3], opening)
     read_out(3, 0, js[3], opening, every)
-    copies3 = project(3, list(range(NCH)), functools.partial(join, 3))
-    sent += list(copies3.values())
+    sent += list(project([(3, n) for n in range(NCH)], join).values())
     for copy in sent:
         copy.wait_send()
     for i in range(NCH):

time: 76.4 us -> 76.1 us (level)
  no operation moved by 1% of the time
where the time goes in v8:
time: 76.1 us; the launch traced here: 75.9 us
  Pallas kernels  75.1 us (99%)
  local copies, waits for them, and re-layouts  0.8 us (1%)
    pallas_call x1, Pallas kernels, body(): pl.pallas_call(functools.partial(kernel, ny, nz, nx), out_shape=jax.Shape...  75.1 us

profile of v8, /device:TPU:1, one launch (start us, length us, event | category | flops | bytes accessed | tf_op | source)
XLA Modules:
  0.0 75.9 jit_solution(4237329332749713167)
XLA Ops:
  0.0 75.1 %shard_map.64 = bf16[64,4096]{1,0:T(8,128)(2,1)S(1)} custom-call(bf16[512,512]{1,0:T(8,128)(2,1)} %q_hbm.1, bf16[512,512]{1,0:T(8,128)(2,1)} %k_hbm.1, bf16[512,512]{1,0:T(8,128)(2,1)} %v_hbm.1, f32[4,512]{1,0:T(4,128)} %bitcast.2, f32[1,512]{1,0:T(1,128)} %bitcast.3, bf16[512,4096]{1,0:T(8,128)(2,1)} %w_hbm.1), custom_call_target="tpu_custom_call" | custom-call | tf_op jit(solution)/shard_map/pallas_call | solution.py:572
  75.1 0.8 %copy.8 = bf16[64,4096]{1,0:T(8,128)(2,1)} copy(bf16[64,4096]{1,0:T(8,128)(2,1)S(1)} %shard_map.64) | data formatting | bytes 1048576

commit v9 on v8

--- a/solution.py
+++ b/solution.py
@@ -16,7 +16,7 @@
 UNROLL = 3
 FULL = 6
 LAG = 4
-PAIR = 2
+PAIR = 4
 HL = 4
 NJ = 4
 NCH = 8

time: 76.1 us -> 76.6 us (level)
  no operation moved by 1% of the time
where the time goes in v9:
time: 76.6 us; the launch traced here: 76.5 us
  Pallas kernels  75.7 us (99%)
  local copies, waits for them, and re-layouts  0.8 us (1%)
    pallas_call x1, Pallas kernels, body(): pl.pallas_call(functools.partial(kernel, ny, nz, nx), out_shape=jax.Shape...  75.7 us

profile of v9, /device:TPU:1, one launch (start us, length us, event | category | flops | bytes accessed | tf_op | source)
XLA Modules:
  0.0 76.5 jit_solution(16358858798664420834)
XLA Ops:
  0.0 75.7 %shard_map.64 = bf16[64,4096]{1,0:T(8,128)(2,1)S(1)} custom-call(bf16[512,512]{1,0:T(8,128)(2,1)} %q_hbm.1, bf16[512,512]{1,0:T(8,128)(2,1)} %k_hbm.1, bf16[512,512]{1,0:T(8,128)(2,1)} %v_hbm.1, f32[4,512]{1,0:T(4,128)} %bitcast.2, f32[1,512]{1,0:T(1,128)} %bitcast.3, bf16[512,4096]{1,0:T(8,128)(2,1)} %w_hbm.1), custom_call_target="tpu_custom_call" | custom-call | tf_op jit(solution)/shard_map/pallas_call | solution.py:572
  75.7 0.8 %copy.8 = bf16[64,4096]{1,0:T(8,128)(2,1)} copy(bf16[64,4096]{1,0:T(8,128)(2,1)S(1)} %shard_map.64) | data formatting | bytes 1048576
